TPU v7x, 32 devices: a whole 2x2x4 slice. The times are simulated.
32 devices in a mesh: dp: 8 (over z, x), tensor: 4 (over y, core).
Axes of the slice: x: 2, y: 2, z: 4, core: 2. Of those that a mesh axis runs over, the one named last changes fastest.
Arguments:
- tokens: bfloat16 [2, 2048, 1024], P(None, 'dp'), may hold values from -6 to 6
- ln1_gain: bfloat16 [1024], replicated, may hold values from 0.5 to 1.5
- ln1_bias: bfloat16 [1024], replicated, may hold values from -0.625 to 0.625
- w_qkv: bfloat16 [1024, 3, 1024], P(None, None, 'tensor'), may hold values from -0.1875 to 0.1875
- qv_bias: bfloat16 [2, 1024], P(None, 'tensor'), may hold values from -0.625 to 0.625
- w_out: bfloat16 [1024, 1024], P('tensor'), may hold values from -2 to 2
- out_bias: bfloat16 [1024], replicated, may hold values from -0.625 to 0.625
- ln2_gain: bfloat16 [1024], replicated, may hold values from 0.5 to 1.5
- ln2_bias: bfloat16 [1024], replicated, may hold values from -0.625 to 0.625
- router: bfloat16 [1024, 2], replicated, may hold values from -0.125 to 0.125
- w_in: bfloat16 [2, 1024, 4096], P(None, None, 'tensor'), may hold values from -0.1875 to 0.1875
- in_bias: bfloat16 [2, 4096], P(None, 'tensor'), may hold values from -0.625 to 0.625
- w_back: bfloat16 [2, 4096, 1024], P(None, 'tensor'), may hold values from -0.1875 to 0.1875
- back_bias: bfloat16 [2, 1024], replicated, may hold values from -0.875 to 0.875
- routes: int32 [2, 2048, 1], P(None, 'dp'), may hold values from 0 to 1, as said below
- prefix: int32 [2], replicated, may hold values from 204 to 1024
- cotangent: bfloat16 [2, 2048, 1024], P(None, 'dp'), may hold values from -6 to 6
Outputs:
- result: float32 [2, 2048, 1024], P(None, 'dp')
- input_grad: float32 [2, 2048, 1024], P(None, 'dp')
- grad_ln1_gain: float32 [1024], replicated
- grad_ln1_bias: float32 [1024], replicated
- grad_w_qkv: float32 [1024, 3, 1024], P(None, None, 'tensor')
- grad_qv_bias: float32 [2, 1024], P(None, 'tensor')
- grad_w_out: float32 [1024, 1024], P('tensor')
- grad_out_bias: float32 [1024], replicated
- grad_ln2_gain: float32 [1024], replicated
- grad_ln2_bias: float32 [1024], replicated
- grad_router: float32 [1024, 2], replicated
- grad_w_in: float32 [2, 1024, 4096], P(None, None, 'tensor')
- grad_in_bias: float32 [2, 4096], P(None, 'tensor')
- grad_w_back: float32 [2, 4096, 1024], P(None, 'tensor')
- grad_back_bias: float32 [2, 1024], replicated
Inputs may be any that keep to these rules, and one draw needn't show every extreme that they name: `routes`: each token names one expert; every expert is named by some token.
All inputs are finite; a program needn't handle non-finite values.
Results may differ from a plain program's by a relative error of at most 0.04.
Values may be sent and summed in bfloat16 or wider, within the bound.
A program may use at most 192 MiB of HBM per device.

v0:
```python
from functools import partial
import math

import jax
import jax.numpy as jnp
from jax import lax
from jax.sharding import PartitionSpec as P

HEAD_DIM = 64
CAP = 320


SCALE = 0.125
EPSILON = 1e-05
MASKED = -1e30
HIGHEST = lax.Precision.HIGHEST


def layer_norm(values, norm_gain, norm_bias):
    centred = values - jnp.mean(values, axis=-1, keepdims=True)
    spread = jnp.mean(centred * centred, axis=-1, keepdims=True)
    return centred * lax.rsqrt(spread + EPSILON) * norm_gain + norm_bias


def heads_of(block, head_count):
    seq_count, row_count, feat_count = block.shape
    return block.reshape(seq_count, row_count, head_count, feat_count // head_count).transpose(
        0, 2, 1, 3
    )


def tokens_of(block):
    seq_count, head_count, row_count, head_width = block.shape
    return block.transpose(0, 2, 1, 3).reshape(seq_count, row_count, head_count * head_width)


def masked_scores(queries, key_heads, query_start, key_start, prefix):
    scores = (
        jnp.einsum("shqd,shkd->shqk", queries, key_heads, preferred_element_type=jnp.float32)
        * SCALE
    )
    query_pos = query_start + jnp.arange(queries.shape[2], dtype=jnp.int32)
    key_pos = key_start + jnp.arange(key_heads.shape[2], dtype=jnp.int32)
    visible_mask = (key_pos[None, None, :] <= query_pos[None, :, None]) | (
        key_pos[None, None, :] < prefix[:, None, None]
    )
    visible_mask = visible_mask[:, None]
    return (jnp.where(visible_mask, scores, MASKED), visible_mask)


def block_live(key_start, query_last, prefix):
    return jnp.any(key_start < prefix) | (key_start <= query_last)


def prob_grads(
    queries, key_heads, value_heads, douts, log_total, delta, query_start, key_start, prefix
):
    scores, visible_mask = masked_scores(queries, key_heads, query_start, key_start, prefix)
    probs = jnp.where(visible_mask, jnp.exp(scores - log_total[..., None]), 0.0)
    dprob = jnp.einsum("shqd,shkd->shqk", douts, value_heads, preferred_element_type=jnp.float32)
    dscore = (probs * (dprob - delta[..., None])).astype(jnp.bfloat16)
    return (probs, dscore)


def attend_fold(run_state, piece_rows, piece_start, queries, first_row, prefix):
    key_piece, value_piece = piece_rows
    head_count = queries.shape[1]
    row_count = key_piece.shape[1]
    block_width = math.gcd(row_count, 512)
    query_last = first_row + queries.shape[2] - 1

    def attend_update(block_index, state_now):
        key_start = block_index * block_width
        key_heads = heads_of(
            lax.dynamic_slice_in_dim(key_piece, block_index * block_width, block_width, 1),
            head_count,
        )
        value_heads = heads_of(
            lax.dynamic_slice_in_dim(value_piece, block_index * block_width, block_width, 1),
            head_count,
        )
        scores, visible_mask = masked_scores(queries, key_heads, first_row, key_start, prefix)
        run_max, run_sum, run_out = state_now
        new_max = jnp.maximum(run_max, jnp.max(scores, axis=-1))
        factor = jnp.exp(run_max - new_max)
        weights = jnp.where(visible_mask, jnp.exp(scores - new_max[..., None]), 0.0)
        run_sum = factor * run_sum + jnp.sum(weights, axis=-1)
        run_out = factor[..., None] * run_out + jnp.einsum(
            "shqk,shkd->shqd", weights, value_heads.astype(jnp.float32), precision=HIGHEST
        )
        return (new_max, run_sum, run_out)

    def attend_block_step(state_now, block_index):
        key_start = block_index * block_width
        is_live = block_live(key_start, query_last, prefix)
        return (
            lax.cond(
                is_live, partial(attend_update, block_index), lambda unchanged: unchanged, state_now
            ),
            None,
        )

    run_state, unused = lax.scan(
        attend_block_step, run_state, jnp.arange(row_count // block_width, dtype=jnp.int32)
    )
    return run_state


def key_pass(queries, douts, log_total, delta, keys_all, values_all, first_row, prefix):
    head_count = queries.shape[1]
    total_rows = keys_all.shape[1]
    block_width = math.gcd(total_rows, 512)
    query_last = first_row + queries.shape[2] - 1

    def key_block_step(dquery, block_index):
        key_start = block_index * block_width

        def work(dquery_now):
            key_heads = heads_of(
                lax.dynamic_slice_in_dim(keys_all, key_start, block_width, 1), head_count
            )
            value_heads = heads_of(
                lax.dynamic_slice_in_dim(values_all, key_start, block_width, 1), head_count
            )
            probs, dscore = prob_grads(
                queries,
                key_heads,
                value_heads,
                douts,
                log_total,
                delta,
                first_row,
                key_start,
                prefix,
            )
            dquery_now = (
                dquery_now
                + jnp.einsum(
                    "shqk,shkd->shqd", dscore, key_heads, preferred_element_type=jnp.float32
                )
                * SCALE
            )
            return (dquery_now, ())

        def skipped(dquery_now):
            return (dquery_now, ())

        return lax.cond(block_live(key_start, query_last, prefix), work, skipped, dquery)

    dquery, key_parts = lax.scan(
        key_block_step,
        jnp.zeros(queries.shape, jnp.float32),
        jnp.arange(total_rows // block_width, dtype=jnp.int32),
    )
    return (dquery, ())


def query_fold(run_state, piece_rows, piece_start, key_heads, value_heads, first_row, prefix):
    query_piece, dout_piece, total_piece, delta_piece = piece_rows
    head_count = key_heads.shape[1]
    row_count = query_piece.shape[1]
    block_width = math.gcd(row_count, 512)

    def query_update(block_index, state_now):
        query_start = block_index * block_width
        offset = block_index * block_width
        queries = heads_of(
            lax.dynamic_slice_in_dim(query_piece, offset, block_width, 1), head_count
        )
        douts = heads_of(lax.dynamic_slice_in_dim(dout_piece, offset, block_width, 1), head_count)
        log_total = lax.dynamic_slice_in_dim(total_piece, offset, block_width, 1).transpose(0, 2, 1)
        delta = lax.dynamic_slice_in_dim(delta_piece, offset, block_width, 1).transpose(0, 2, 1)
        probs, dscore = prob_grads(
            queries, key_heads, value_heads, douts, log_total, delta, query_start, first_row, prefix
        )
        dkey_now, dvalue_now = state_now
        dkey_now = (
            dkey_now
            + jnp.einsum("shqk,shqd->shkd", dscore, queries, preferred_element_type=jnp.float32)
            * SCALE
        )
        dvalue_now = dvalue_now + jnp.einsum(
            "shqk,shqd->shkd", probs, douts.astype(jnp.float32), precision=HIGHEST
        )
        return (dkey_now, dvalue_now)

    def query_block_step(state_now, block_index):
        query_last = block_index * block_width + block_width - 1
        is_live = block_live(first_row, query_last, prefix)
        return (
            lax.cond(
                is_live, partial(query_update, block_index), lambda unchanged: unchanged, state_now
            ),
            None,
        )

    run_state, unused = lax.scan(
        query_block_step, run_state, jnp.arange(row_count // block_width, dtype=jnp.int32)
    )
    return run_state


def local(
    tokens,
    ln1_gain,
    ln1_bias,
    w_qkv,
    qv_bias,
    w_out,
    out_bias,
    ln2_gain,
    ln2_bias,
    router,
    w_in,
    in_bias,
    w_back,
    back_bias,
    routes,
    prefix,
    cotangent,
):
    seq_count, span_len, model_width = tokens.shape
    tok_rows = seq_count * span_len
    local_feats = w_qkv.shape[2]
    head_count = local_feats // HEAD_DIM
    expert_count = w_in.shape[0]
    first_row = lax.axis_index("dp") * span_len
    local_shape = (seq_count, span_len, local_feats)
    source = tokens.reshape(tok_rows, model_width).astype(jnp.float32)
    normed_one, ln1_pull = jax.vjp(
        layer_norm, source, ln1_gain.astype(jnp.float32), ln1_bias.astype(jnp.float32)
    )
    hidden_one = normed_one.astype(jnp.bfloat16)
    projected = jnp.einsum("ti,icf->tcf", hidden_one, w_qkv, preferred_element_type=jnp.float32)
    bias_float = qv_bias.astype(jnp.float32)
    query_tok = (projected[:, 0] + bias_float[0]).astype(jnp.bfloat16).reshape(local_shape)
    key_tok = projected[:, 1].astype(jnp.bfloat16).reshape(local_shape)
    value_tok = (projected[:, 2] + bias_float[1]).astype(jnp.bfloat16).reshape(local_shape)
    queries = heads_of(query_tok, head_count)
    stat_shape = queries.shape[:3]
    start_state = (
        jnp.full(stat_shape, MASKED, jnp.float32),
        jnp.zeros(stat_shape, jnp.float32),
        jnp.zeros(queries.shape, jnp.float32),
    )
    fold_keys = partial(attend_fold, queries=queries, first_row=first_row, prefix=prefix)
    run_max, run_sum, run_out = fold_keys(
        start_state,
        (
            lax.all_gather(key_tok, "dp", axis=1, tiled=True),
            lax.all_gather(value_tok, "dp", axis=1, tiled=True),
        ),
        jnp.int32(0),
    )
    mixed_heads = run_out / run_sum[..., None]
    log_total = run_max + jnp.log(run_sum)
    mixed_b = tokens_of(mixed_heads.astype(jnp.bfloat16)).reshape(tok_rows, local_feats)
    out_shift = out_bias.astype(jnp.float32)
    gain_two = ln2_gain.astype(jnp.float32)
    shift_two = ln2_bias.astype(jnp.float32)
    attn_part = jnp.dot(mixed_b, w_out, preferred_element_type=jnp.float32)
    attn_out = lax.psum(attn_part, "tensor") + out_shift
    residual = source + attn_out
    normed_two, ln2_pull = jax.vjp(layer_norm, residual, gain_two, shift_two)
    hidden_two = normed_two.astype(jnp.bfloat16)
    logits = jnp.dot(hidden_two, router, preferred_element_type=jnp.float32)
    chosen = routes.reshape(tok_rows)
    expert_ids = jnp.arange(expert_count, dtype=jnp.int32)
    expert_hot = (chosen[:, None] == expert_ids[None, :]).astype(jnp.int32)

    def gate_of(logit_vals):
        return jnp.sum(
            jnp.where(expert_hot == 1, jax.nn.softmax(logit_vals, axis=-1), 0.0), axis=-1
        )

    gate_value, gate_pull = jax.vjp(gate_of, logits)
    earlier = jnp.cumsum(expert_hot, axis=0, dtype=jnp.int32) - expert_hot
    slot_place = jnp.sum(earlier * expert_hot, axis=1, dtype=jnp.int32)
    slot_ids = jnp.arange(CAP, dtype=jnp.int32)
    select_mask = (expert_hot[:, :, None] == 1) & (
        slot_place[:, None, None] == slot_ids[None, None, :]
    )
    select = select_mask.astype(jnp.bfloat16)
    select_float = select_mask.astype(jnp.float32)
    dispatched = jnp.einsum(
        "tec,td->ecd", select, hidden_two, preferred_element_type=jnp.float32
    ).astype(jnp.bfloat16)
    pre_act = (
        jnp.einsum("ecd,edf->ecf", dispatched, w_in, preferred_element_type=jnp.float32)
        + in_bias.astype(jnp.float32)[:, None, :]
    )
    act_float, gelu_pull = jax.vjp(partial(jax.nn.gelu, approximate=False), pre_act)
    active = act_float.astype(jnp.bfloat16)
    expert_part = jnp.einsum("ecf,efd->ecd", active, w_back, preferred_element_type=jnp.float32)
    expert_full = lax.psum(expert_part, "tensor") + back_bias.astype(jnp.float32)[:, None, :]
    combined = jnp.einsum("tec,ecd->td", select_float, expert_full, precision=HIGHEST)
    layer_rows = residual + gate_value[:, None] * combined
    grad_out = cotangent.reshape(tok_rows, model_width).astype(jnp.float32)
    dgate = jnp.sum(grad_out * combined, axis=-1)
    dlogit_b = gate_pull(dgate)[0].astype(jnp.bfloat16)
    gated_grad = (gate_value[:, None] * grad_out).astype(jnp.bfloat16)
    dexpert_b = jnp.einsum(
        "tec,td->ecd", select, gated_grad, preferred_element_type=jnp.float32
    ).astype(jnp.bfloat16)
    grad_back_bias = jnp.sum(dexpert_b, axis=1, dtype=jnp.float32)
    grad_w_back = jnp.einsum("ecf,ecd->efd", active, dexpert_b, preferred_element_type=jnp.float32)
    dactive = jnp.einsum("ecd,efd->ecf", dexpert_b, w_back, preferred_element_type=jnp.float32)
    dpre_b = gelu_pull(dactive)[0].astype(jnp.bfloat16)
    grad_in_bias = jnp.sum(dpre_b, axis=1, dtype=jnp.float32)
    grad_w_in = jnp.einsum("ecd,ecf->edf", dispatched, dpre_b, preferred_element_type=jnp.float32)
    slot_part = jnp.einsum("ecf,edf->ecd", dpre_b, w_in, preferred_element_type=jnp.float32)
    dslots = lax.psum(slot_part, "tensor")
    dnorm_two = jnp.einsum("tec,ecd->td", select_float, dslots, precision=HIGHEST) + jnp.einsum(
        "te,de->td", dlogit_b, router, preferred_element_type=jnp.float32
    )
    grad_router = jnp.einsum("td,te->de", hidden_two, dlogit_b, preferred_element_type=jnp.float32)
    dresid_norm, grad_ln2_gain, grad_ln2_bias = ln2_pull(dnorm_two)
    dresidual = grad_out + dresid_norm
    dattn_b = dresidual.astype(jnp.bfloat16)
    grad_out_bias = jnp.sum(dattn_b, axis=0, dtype=jnp.float32)
    grad_w_out = jnp.einsum("tf,td->fd", mixed_b, dattn_b, preferred_element_type=jnp.float32)
    dmixed_tok = (
        jnp.einsum("td,fd->tf", dattn_b, w_out, preferred_element_type=jnp.float32)
        .astype(jnp.bfloat16)
        .reshape(local_shape)
    )
    douts = heads_of(dmixed_tok, head_count)
    delta = jnp.sum(douts.astype(jnp.float32) * mixed_heads, axis=-1)
    keys_all, values_all = (
        lax.all_gather(key_tok, "dp", axis=1, tiled=True),
        lax.all_gather(value_tok, "dp", axis=1, tiled=True),
    )
    dquery, unused = key_pass(
        queries, douts, log_total, delta, keys_all, values_all, first_row, prefix
    )
    total_rows = log_total.transpose(0, 2, 1)
    delta_rows = delta.transpose(0, 2, 1)
    fold_rows = partial(
        query_fold,
        key_heads=heads_of(key_tok, head_count),
        value_heads=heads_of(value_tok, head_count),
        first_row=first_row,
        prefix=prefix,
    )
    zero_heads = jnp.zeros(queries.shape, jnp.float32)
    dkey_heads, dvalue_heads = fold_rows(
        (zero_heads, zero_heads),
        (
            lax.all_gather(query_tok, "dp", axis=1, tiled=True),
            lax.all_gather(dmixed_tok, "dp", axis=1, tiled=True),
            lax.all_gather(total_rows.astype(jnp.bfloat16), "dp", axis=1, tiled=True).astype(
                jnp.float32
            ),
            lax.all_gather(delta_rows.astype(jnp.bfloat16), "dp", axis=1, tiled=True).astype(
                jnp.float32
            ),
        ),
        jnp.int32(0),
    )
    dkey = tokens_of(dkey_heads)
    dvalue = tokens_of(dvalue_heads)
    dquery_b = tokens_of(dquery).astype(jnp.bfloat16).reshape(tok_rows, local_feats)
    dkey_b = dkey.astype(jnp.bfloat16).reshape(tok_rows, local_feats)
    dvalue_b = dvalue.astype(jnp.bfloat16).reshape(tok_rows, local_feats)
    dproject = jnp.stack([dquery_b, dkey_b, dvalue_b], axis=1)
    grad_qv_bias = jnp.stack(
        [jnp.sum(dquery_b, axis=0, dtype=jnp.float32), jnp.sum(dvalue_b, axis=0, dtype=jnp.float32)]
    )
    grad_w_qkv = jnp.einsum("ti,tcf->icf", hidden_one, dproject, preferred_element_type=jnp.float32)
    norm_part = jnp.einsum("tcf,icf->ti", dproject, w_qkv, preferred_element_type=jnp.float32)
    dnorm_one = lax.psum(norm_part, "tensor")
    dsource_norm, grad_ln1_gain, grad_ln1_bias = ln1_pull(dnorm_one)
    input_grad = (dresidual + dsource_norm).reshape(seq_count, span_len, model_width)
    summed = lax.psum(
        (
            grad_ln1_gain,
            grad_ln1_bias,
            grad_w_qkv,
            grad_qv_bias,
            grad_w_out,
            grad_out_bias,
            grad_ln2_gain,
            grad_ln2_bias,
            grad_router,
            grad_w_in,
            grad_in_bias,
            grad_w_back,
            grad_back_bias,
        ),
        "dp",
    )
    layer_out = layer_rows.reshape(seq_count, span_len, model_width)
    return (layer_out, input_grad) + tuple(summed)


def solution(mesh):
    in_specs = (
        P(None, "dp", None),
        P(),
        P(),
        P(None, None, "tensor"),
        P(None, "tensor"),
        P("tensor", None),
        P(),
        P(),
        P(),
        P(),
        P(None, None, "tensor"),
        P(None, "tensor"),
        P(None, "tensor", None),
        P(),
        P(None, "dp", None),
        P(),
        P(None, "dp", None),
    )
    out_specs = (
        P(None, "dp", None),
        P(None, "dp", None),
        P(),
        P(),
        P(None, None, "tensor"),
        P(None, "tensor"),
        P("tensor", None),
        P(),
        P(),
        P(),
        P(),
        P(None, None, "tensor"),
        P(None, "tensor"),
        P(None, "tensor", None),
        P(),
    )
    return jax.shard_map(local, mesh=mesh, in_specs=in_specs, out_specs=out_specs, check_vma=False)
```

profile of v0, /device:TPU:0, one launch (start us, length us, event | category | flops | bytes accessed | tf_op | source)
XLA Modules:
  0.0 1290.9 jit_solution(3859642581222658883)
XLA Ops:
  26.9 42.4 %all-gather.5.cloned.1.call-done = bf16[2,2048,256]{1,2,0:T(8,128)(2,1)} async-done(((bf16[2,256,256]{1,2,0:T(8,128)(2,1)}), bf16[2,2048,256]{1,2,0:T(8,128)(2,1)}) %all-gather.5.cloned.1.call-update) | async-done | bytes 2097168 | tf_op jit(solution)/shard_map/all_gather | solution.py:250
  69.3 51.2 %all-gather.7.cloned.1.call-done = bf16[2,2048,256]{1,2,0:T(8,128)(2,1)} async-done(((bf16[2,256,256]{1,2,0:T(8,128)(2,1)}), bf16[2,2048,256]{1,2,0:T(8,128)(2,1)}) %all-gather.7.cloned.1.call-update) | async-done | bytes 2097168 | tf_op jit(solution)/shard_map/all_gather | solution.py:251
  121.3 26.1 %while.44 = (s32[]{:T(128)}, f32[2,4,256]{2,1,0:T(4,128)S(1)}, f32[2,4,256]{2,1,0:T(4,128)S(1)}, f32[2,4,256,64]{2,3,1,0:T(8,128)}, s32[4]{0:T(128)S(1)}, /*inde...) while((s32[]{:T(128)}, f32[2,4,256]{2,1,0:T(4,128)S(1)}, ...), condition=%wide.region_8.9_spmd, body=%wide.region_2.8_spmd.sunk | while | flops 952768256 | bytes 22686132 | solution.py:103
  123.8 7.9 conditional.6
  134.3 7.9 conditional.6
  155.6 63.2 %all-reduce.8.cloned.1.call-done = f32[512,1024]{1,0:T(8,128)} async-done(((f32[512,1024]{1,0:T(8,128)}), f32[512,1024]{1,0:T(8,128)}) %all-reduce.8.cloned.1.call-update) | async-done | bytes 2097168 | tf_op jit(solution)/shard_map/psum | solution.py:262
  226.3 7.0 multiply_convert_fusion.1
  239.8 57.8 %all-reduce.10.cloned.1.call-done = f32[2,320,1024]{2,1,0:T(8,128)} async-done(((f32[2,320,1024]{2,1,0:T(8,128)}), f32[2,320,1024]{2,1,0:T(8,128)}) %all-reduce.10.cloned.1.call-update) | async-done | bytes 2621456 | tf_op jit(solution)/shard_map/psum | solution.py:295
  297.6 6.3 fusion.54
  319.0 54.1 %all-reduce.12.cloned.1.call-done = f32[2,320,1024]{2,1,0:T(8,128)} async-done(((f32[2,320,1024]{2,1,0:T(8,128)}), f32[2,320,1024]{2,1,0:T(8,128)}) %all-reduce.12.cloned.1.call-update) | async-done | bytes 2621456 | tf_op jit(solution)/shard_map/psum | solution.py:312
  373.1 7.0 multiply_reduce_fusion
  394.6 26.4 %all_gather.23 = bf16[2,2048,4]{1,2,0:T(4,128)(2,1)S(1)} all-gather(bf16[2,256,4]{1,2,0:T(4,128)(2,1)S(1)} %get-tuple-element.754), channel_id=1, replica_groups=mesh['dp'=8,'tensor'=4] {'dp'}, dimensions={1}, use_global_device_ids=true | all-gather | bytes 36864 | tf_op jit(solution)/shard_map/all_gather | solution.py:351
  421.0 7.5 fusion.129
  430.8 19.9 %all_gather.25 = bf16[2,2048,4]{1,0,2:T(2,128)(2,1)S(1)} all-gather(bf16[2,256,4]{1,0,2:T(2,128)(2,1)S(1)} %convert_bitcast_fusion.3), channel_id=1, replica_groups=mesh['dp'=8,'tensor'=4] {'dp'}, dimensions={1}, use_global_device_ids=true | all-gather | bytes 36864 | tf_op jit(solution)/shard_map/all_gather | solution.py:354
  452.2 33.7 %while.45 = (s32[]{:T(128)}, f32[2,4,256,64]{2,3,1,0:T(8,128)}, s32[4]{0:T(128)S(1)}, s32[2]{0:T(128)S(1)}, s32[]{:T(128)}, /*index=5*/s32[]{:T(128)}, bf16[2,20...) while((s32[]{:T(128)}, f32[2,4,256,64]{2,3,1,0:T(8,128)}, ...), condition=%wide.region_29.30_spmd, body=%wide.region_25.29_spmd.sunk | while | flops 410650368 | bytes 14444881 | solution.py:150
  454.7 11.8 conditional.7
  469.1 11.8 conditional.7
  489.9 85.5 %while.46 = (s32[]{:T(128)}, f32[2,4,256,64]{2,3,1,0:T(8,128)S(1)}, f32[2,4,256,64]{2,3,1,0:T(8,128)}, s32[4]{0:T(128)}, s32[]{:T(128)}, /*index=5*/pred[]{:T(51...) while((s32[]{:T(128)}, f32[2,4,256,64]{2,3,1,0:T(8,128)S(1)}, ...), condition=%wide.region_34.35_spmd, body=%wide.region_31.34_spmd.sunk | while | flops 1220281600 | bytes 26862088 | solution.py:197
  492.5 18.8 %conditional.8 = ((f32[2,4,256,64]{2,3,1,0:T(8,128)S(1)}, f32[2,4,256,64]{2,3,1,0:T(8,128)})) conditional(s32[]{:T(128)} %convert_element_type.396, (f32[2,4,256,64]{2,3,1,0:T(8,128)S(1)}, f32[2,4,256,64]{2,3,1,0:T(8,128)}) %tuple.136, (s32[]{:T(128)}, s32[]{:T(128)}, s32[2]{0:T(128)S(1)}, bf16[2,2048,256]{1,2,0:T(8,128)(2,1)}, ...), branch_computations={%region_32.32_spmd, %region_33.33_spmd} | conditional | flops 1220281600 | bytes 26861774 | solution.py:191
  499.9 5.3 fusion.30
  505.2 6.0 fusion.31
  513.9 18.8 %conditional.8 = ((f32[2,4,256,64]{2,3,1,0:T(8,128)S(1)}, f32[2,4,256,64]{2,3,1,0:T(8,128)})) conditional(s32[]{:T(128)} %convert_element_type.396, (f32[2,4,256,64]{2,3,1,0:T(8,128)S(1)}, f32[2,4,256,64]{2,3,1,0:T(8,128)}) %tuple.136, (s32[]{:T(128)}, s32[]{:T(128)}, s32[2]{0:T(128)S(1)}, bf16[2,2048,256]{1,2,0:T(8,128)(2,1)}, ...), branch_computations={%region_32.32_spmd, %region_33.33_spmd} | conditional | flops 1220281600 | bytes 26861774 | solution.py:191
  526.6 6.0 fusion.31
  535.2 18.8 %conditional.8 = ((f32[2,4,256,64]{2,3,1,0:T(8,128)S(1)}, f32[2,4,256,64]{2,3,1,0:T(8,128)})) conditional(s32[]{:T(128)} %convert_element_type.396, (f32[2,4,256,64]{2,3,1,0:T(8,128)S(1)}, f32[2,4,256,64]{2,3,1,0:T(8,128)}) %tuple.136, (s32[]{:T(128)}, s32[]{:T(128)}, s32[2]{0:T(128)S(1)}, bf16[2,2048,256]{1,2,0:T(8,128)(2,1)}, ...), branch_computations={%region_32.32_spmd, %region_33.33_spmd} | conditional | flops 1220281600 | bytes 26861774 | solution.py:191
  548.0 6.0 fusion.31
  556.6 18.8 %conditional.8 = ((f32[2,4,256,64]{2,3,1,0:T(8,128)S(1)}, f32[2,4,256,64]{2,3,1,0:T(8,128)})) conditional(s32[]{:T(128)} %convert_element_type.396, (f32[2,4,256,64]{2,3,1,0:T(8,128)S(1)}, f32[2,4,256,64]{2,3,1,0:T(8,128)}) %tuple.136, (s32[]{:T(128)}, s32[]{:T(128)}, s32[2]{0:T(128)S(1)}, bf16[2,2048,256]{1,2,0:T(8,128)(2,1)}, ...), branch_computations={%region_32.32_spmd, %region_33.33_spmd} | conditional | flops 1220281600 | bytes 26861774 | solution.py:191
  569.4 6.0 fusion.31
  586.3 7.9 fusion.130
  600.2 33.6 %all-reduce.14.cloned.1.call-done = f32[512,1024]{1,0:T(8,128)} async-done(((f32[512,1024]{1,0:T(8,128)}), f32[512,1024]{1,0:T(8,128)}) %all-reduce.14.cloned.1.call-update) | async-done | bytes 2097168 | tf_op jit(solution)/shard_map/psum | solution.py:371
  637.2 40.5 %all-reduce = (f32[1024]{0:T(1024)}, f32[1024]{0:T(1024)}, f32[2,256]{1,0:T(2,128)}, f32[1024]{0:T(1024)}, f32[1024]{0:T(1024)}, /*index=5*/f32[1024]{0:T(1024)}...) all-reduce(f32[1024]{0:T(1024)S(1)} %get-tuple-element.652, ...), channel_id=1, replica_groups=mesh['dp'=8,'tensor'=4] {'dp'}, use_global_device_ids=true, to_apply=%region_39.40 | all-reduce | flops 11776 | bytes 94208 | tf_op jit(solution)/shard_map/psum | solution.py:374
  682.6 584.0 %all-reduce.16.cloned.1.call-done = (f32[1024,3,256]{2,0,1:T(8,128)}, f32[256,1024]{1,0:T(8,128)}, f32[2,1024,1024]{2,1,0:T(8,128)}, f32[2,1024,1024]{2,1,0:T(8,128)}) async-done(((f32[1024,3,256]{2,0,1:T(8,128)}, f32[256,1024]{1,0:T(8,128)}, f32[2,1024,1024]{2,1,0:T(8,128)}, f32[2,1024,1024]{2,1,0:T(8,128)}), (f32[1024,3,256]{2,0,1:T(8,128)}, f32[256,1024]{1,0:T(8,128)}, f32[2,1024,1024]{2,1,0:T(8,128)}, ...) | async-done | bytes 20971536 | tf_op jit(solution)/shard_map/psum | solution.py:374
  1271.4 9.1 copy.165
  (391 shorter events, 208.3 us)
Async XLA Ops:
  7.2 62.1 %all-gather.5.cloned.1.call-start = ((), (), s32[]{:S(2)}) async-start(), calls=%async_computation | async-start | bytes 2359296 | tf_op jit(solution)/shard_map/all_gather | solution.py:250
  15.2 8.1 copy-start.19
  15.2 6.1 copy-start.54
  15.2 6.1 copy-start.55
  16.0 104.4 %all-gather.7.cloned.1.call-start = ((), (), s32[]{:S(2)}) async-start(), calls=%async_computation.1 | async-start | bytes 2359296 | tf_op jit(solution)/shard_map/all_gather | solution.py:251
  19.2 102.1 %copy-start.37 = (s32[2]{0:T(128)S(1)}, s32[2]{0:T(128)}, u32[]{:S(2)}) copy-start(s32[2]{0:T(128)} %param.44) | copy-start | bytes 28
  21.1 197.7 %all-reduce.8.cloned.1.call-start = ((), (), s32[]{:S(2)}) async-start(), calls=%async_computation.2 | async-start | bytes 4194304 | tf_op jit(solution)/shard_map/psum | solution.py:262
  153.3 144.3 %all-reduce.10.cloned.1.call-start = ((), (), s32[]{:S(2)}) async-start(), calls=%async_computation.3 | async-start | bytes 5242880 | tf_op jit(solution)/shard_map/psum | solution.py:295
  226.3 7.0 copy-start.16
  226.3 8.1 copy-start.56
  237.5 135.7 %all-reduce.12.cloned.1.call-start = ((), (), s32[]{:S(2)}) async-start(), calls=%async_computation.4 | async-start | bytes 5242880 | tf_op jit(solution)/shard_map/psum | solution.py:312
  297.6 6.4 copy-start.10
  297.6 6.4 copy-start.35
  297.6 8.0 copy-start.18
  297.6 8.0 copy-start.57
  313.0 175.5 %all-gather.9.cloned.1.call-start = ((), (), s32[]{:S(2)}) async-start(), calls=%async_computation.5 | async-start | bytes 2359296 | tf_op jit(solution)/shard_map/all_gather | solution.py:349
  316.9 171.5 %all-gather.11.cloned.1.call-start = ((), (), s32[]{:S(2)}) async-start(), calls=%async_computation.6 | async-start | bytes 2359296 | tf_op jit(solution)/shard_map/all_gather | solution.py:350
  373.1 7.0 copy-start.2
  373.1 7.0 copy-start.27
  386.7 247.1 %all-reduce.14.cloned.1.call-start = ((), (), s32[]{:S(2)}) async-start(), calls=%async_computation.7 | async-start | bytes 4194304 | tf_op jit(solution)/shard_map/psum | solution.py:371
  421.0 7.5 copy-start.33
  586.0 8.2 copy-start.21
  586.0 680.5 %all-reduce.16.cloned.1.call-start = ((), (), s32[]{:S(2)}) async-start(), calls=%async_computation.8 | async-start | bytes 41943040 | tf_op jit(solution)/shard_map/psum | solution.py:374
  586.3 7.9 copy-start.13
  598.5 35.4 %copy-start.39 = (f32[1024]{0:T(1024)S(1)}, f32[1024]{0:T(1024)}, u32[]{:S(2)}) copy-start(f32[1024]{0:T(1024)} %copy-done.38) | copy-start | bytes 12292
  598.5 35.4 %copy-start.42 = (f32[1,2,2,128]{3,1,2,0:T(2,128)S(1)}, f32[1,2,2,128]{3,1,2,0:T(2,128)}, u32[]{:S(2)}) copy-start(f32[1,2,2,128]{3,1,2,0:T(2,128)} %copy-done.41) | copy-start | bytes 6148
  598.5 37.6 %copy-start.46 = (f32[1,2,2,128]{3,1,2,0:T(2,128)S(1)}, f32[1,2,2,128]{3,1,2,0:T(2,128)}, u32[]{:S(2)}) copy-start(f32[1,2,2,128]{3,1,2,0:T(2,128)} %copy-done.45) | copy-start | bytes 6148
  598.5 37.6 %copy-start.44 = (f32[512]{0:T(512)S(1)}, f32[512]{0:T(512)}, u32[]{:S(2)}) copy-start(f32[512]{0:T(512)} %copy-done.43) | copy-start | bytes 6148
  600.2 37.0 %copy-start.49 = (f32[2,1024]{1,0:T(2,128)S(1)}, f32[2,1024]{1,0:T(2,128)}, u32[]{:S(2)}) copy-start(f32[2,1024]{1,0:T(2,128)} %get-tuple-element.791) | copy-start | bytes 24580
  600.2 37.0 %copy-start.50 = (f32[2,1024]{1,0:T(2,128)S(1)}, f32[2,1024]{1,0:T(2,128)}, u32[]{:S(2)}) copy-start(f32[2,1024]{1,0:T(2,128)} %get-tuple-element.750) | copy-start | bytes 24580
  1270.4 10.1 slice-start
  1271.4 9.1 slice-start.1
  (53 other events, 138.8 us)
Sparse Core Ops, SparseCore 0:
  16.2 53.0 all-gather.4
  71.9 48.5 all-gather.6
  153.5 65.3 all-reduce.7
  237.6 59.9 all-reduce.9
  313.1 59.9 all-reduce.11
  375.0 50.7 all-gather.8
  427.8 48.8 all-gather.10
  586.1 47.6 all-reduce.13
  639.9 626.6 all-reduce.15
where the time goes:
time: 1300 us; the launch traced here: 1290 us
  waiting for transfers between devices  886 us (68%)
  matrix products  140 us (11%)
  blocking collectives  86.8 us (7%)
  local copies, waits for them, and re-layouts  86.2 us (7%)
  other arithmetic  54.7 us (4%)
  loops' own time  20.3 us (2%)
  between operations  15 us (1%)
    psum x1, waiting for transfers between devices, local(): lax.psum((grad_ln1_gain, grad_ln1_bias, grad_w_qkv, grad_qv_bias, grad_w_...  584 us
    psum x1, waiting for transfers between devices, local(): attn_out = lax.psum(attn_part, 'tensor') + out_shift  63.2 us
    psum x1, waiting for transfers between devices, local(): lax.psum(expert_part, 'tensor') + back_bias.astype(jnp.float32)[:, None, :]  57.8 us
    psum x1, waiting for transfers between devices, local(): dslots = lax.psum(slot_part, 'tensor')  54.1 us
    all_gather x1, waiting for transfers between devices, local(): lax.all_gather(value_tok, 'dp', axis=1, tiled=True)  51.2 us
    all_gather x1, waiting for transfers between devices, local(): lax.all_gather(key_tok, 'dp', axis=1, tiled=True)  42.4 us
    psum x1, blocking collectives, local(): lax.psum((grad_ln1_gain, grad_ln1_bias, grad_w_qkv, grad_qv_bias, grad_w_...  40.5 us
    psum x1, waiting for transfers between devices, local(): dnorm_one = lax.psum(norm_part, 'tensor')  33.6 us
  transfers between devices with their start and end apart: 9, of which 7 were waited for; matrix products, arithmetic and copies ran while one was open for 8% of the time, Pallas kernels for 0%

commit v1 on v0

--- a/solution.py
+++ b/solution.py
@@ -1,13 +1,1022 @@
-from functools import partial
+import functools
 import math
 
 import jax
 import jax.numpy as jnp
 from jax import lax
+from jax.experimental import pallas as pl
+from jax.experimental.pallas import tpu as pltpu
 from jax.sharding import PartitionSpec as P
 
+F32 = jnp.float32
+BF = jnp.bfloat16
+MESH = pl.DeviceIdType.MESH
+EPS = 1e-05
+CAP = 320
 HEAD_DIM = 64
-CAP = 320
+NEG = -1e30
+CH = 128
+
+
+def mm(a, b):
+    return lax.dot_general(a, b, (((1,), (0,)), ((), ())), preferred_element_type=F32)
+
+
+def mm_bt(a, b):
+    return lax.dot_general(a, b, (((1,), (1,)), ((), ())), preferred_element_type=F32)
+
+
+def mm_at(a, b):
+    return lax.dot_general(a, b, (((0,), (0,)), ((), ())), preferred_element_type=F32)
+
+
+def loop(n, body):
+    def step(i, carry):
+        body(i)
+        return carry
+
+    lax.fori_loop(0, n, step, 0)
+
+
+def al(v, m):
+    return pl.multiple_of(v, m)
+
+
+def lanes(rows):
+    return lax.broadcasted_iota(jnp.int32, (rows, 128), 1)
+
+
+def roll64(v):
+    return pltpu.roll(v, 64, 1)
+
+
+class Ctx:
+    def __init__(self, ssem, rsem, lsem):
+        self.ssem, self.rsem, self.lsem = ssem, rsem, lsem
+        self.next = 0
+        self.pending = []
+        dp = lax.axis_index("dp")
+        t = lax.axis_index("tensor")
+        self.dp, self.t = dp, t
+        self.z, self.x = dp // 2, lax.rem(dp, 2)
+        self.y, self.c = t // 2, lax.rem(t, 2)
+        x1 = 1 - self.x
+        dpx = self.z * 2 + x1
+        tm = self.y * 2 + 1 - self.c
+        ty = (1 - self.y) * 2 + self.c
+        self.mate = (dp, tm)
+        self.yp = (dp, ty)
+        self.xp = (dpx, t)
+        self.dg = (dpx, ty)
+        self.t_mate, self.t_y = tm, ty
+
+    def sems(self, n):
+        k = self.next
+        self.next += n
+        return k
+
+    def rc(self, src, dst, k, dev, kr=None):
+        return pltpu.make_async_remote_copy(
+            src_ref=src,
+            dst_ref=dst,
+            send_sem=self.ssem.at[k],
+            recv_sem=self.rsem.at[k if kr is None else kr],
+            device_id=dev,
+            device_id_type=MESH,
+        )
+
+    def send(self, src, dst, k, dev):
+        cp = self.rc(src, dst, k, dev)
+        cp.start()
+        self.pending.append(cp)
+        return cp
+
+    def drain(self):
+        for cp in self.pending:
+            cp.wait_send()
+        self.pending = []
+
+
+def barrier_start(C, n_dp):
+    sem = pltpu.get_barrier_semaphore()
+    devs = [(lax.rem(C.dp + o, n_dp), C.t) for o in range(1, n_dp)]
+    devs += [C.mate, C.yp, C.dg, (C.dp, 3 - C.t)]
+    for d in devs:
+        pl.semaphore_signal(sem, inc=1, device_id=d, device_id_type=MESH)
+    return sem, len(devs)
+
+
+def norm_parts(v):
+    mean = jnp.mean(v, axis=-1, keepdims=True)
+    cent = v - mean
+    var = jnp.mean(cent * cent, axis=-1, keepdims=True)
+    r = lax.rsqrt(var + EPS)
+    return cent * r, r
+
+
+def stage_qkv(R, C):
+    rows = R.tok.shape[0]
+    gain, bias = R.par[0:1, :], R.par[1:2, :]
+
+    def ln(i):
+        at = pl.ds(al(i * 32, 32), 32)
+        n, _ = norm_parts(R.tok[at, :].astype(F32))
+        R.h1[at, :] = (n * gain + bias).astype(BF)
+
+    loop(rows // 32, ln)
+    hp = R.wqkv.shape[2] // HEAD_DIM
+
+    def seq(s):
+        at = pl.ds(al(s * 256, 256), 256)
+        h = R.h1[at, :]
+        lo = lanes(256) < 64
+        lo2 = lanes(128) < 64
+        for pr in range(hp // 2):
+            cut = slice(pr * 128, pr * 128 + 128)
+            tq = (mm(h, R.wqkv[0, :, cut]) + R.qvb[0:1, cut].astype(F32)) * 0.125
+            tk = mm(h, R.wqkv[1, :, cut])
+            tv = mm(h, R.wqkv[2, :, cut]) + R.qvb[1:2, cut].astype(F32)
+            p = s * hp + 2 * pr
+            R.asend[p, 0:256, :] = jnp.where(lo, tq, roll64(tk)).astype(BF)
+            R.asend[p + 1, 0:256, :] = jnp.where(lo, roll64(tq), tk).astype(BF)
+            a, b = tv[0:128], tv[128:256]
+            R.asend[p, 256:384, :] = jnp.where(lo2, a, roll64(b)).astype(BF)
+            R.asend[p + 1, 256:384, :] = jnp.where(lo2, roll64(a), b).astype(BF)
+
+    loop(rows // 256, seq)
+
+
+def all_to_all(R, C, src, dst, n):
+    k = C.sems(n)
+    cps = [
+        C.send(src.at[lax.rem(C.dp + o, n)], dst.at[C.dp], k + o, (lax.rem(C.dp + o, n), C.t))
+        for o in range(1, n)
+    ]
+    mine = pltpu.make_async_copy(src.at[C.dp], dst.at[C.dp], C.lsem.at[0])
+    mine.start()
+
+    def wait():
+        mine.wait()
+        for cp in cps:
+            cp.wait_recv()
+
+    return wait
+
+
+def stage_attend(R, C, n):
+    lo = lanes(256) < 64
+    lo2 = lanes(128) < 64
+    one = jnp.where((lanes(256) == 64) | (lanes(256) == 65), 1.0, 0.0)
+    one2 = one[0:128]
+
+    def unpack(b):
+        qk = R.arecv[b, 0:256, :].astype(F32)
+        vf = R.arecv[b, 256:384, :].astype(F32)
+        at = pl.ds(al(b * 256, 256), 256)
+        R.Q[at, :] = jnp.where(lo, qk, 0.0).astype(BF)
+        R.K[at, :] = jnp.where(lo, roll64(qk), one).astype(BF)
+        R.V[pl.ds(al(b * 256, 128), 128), :] = jnp.where(lo2, vf, one2).astype(BF)
+        R.V[pl.ds(al(b * 256 + 128, 128), 128), :] = jnp.where(lo2, roll64(vf), one2).astype(BF)
+
+    loop(n, unpack)
+    T = 512
+    half = R.Q.shape[0] // 2 // T - 1
+    seqs = R.prefix.shape[0]
+    prefix = R.prefix[C.dp // (n // seqs)]
+    k = C.sems(n)
+
+    def rows_of(i):
+        at = pl.ds(al(i * T, T), T)
+        q = R.Q[at, :]
+        qpos = i * T + lax.broadcasted_iota(jnp.int32, (T, 1), 0)
+        lim = jnp.maximum(qpos, prefix - 1)
+
+        def tile(j, carry):
+            m, acc = carry
+            kat = pl.ds(al(j * T, T), T)
+            s = mm_bt(q, R.K[kat, :])
+            kpos = j * T + lax.broadcasted_iota(jnp.int32, (T, T), 1)
+            s = jnp.where(kpos <= lim, s, NEG)
+            m2 = jnp.maximum(m, jnp.max(s, axis=1, keepdims=True))
+            p = jnp.exp(s - m2).astype(BF)
+            acc = acc * jnp.exp(m - m2) + mm(p, R.V[kat, :])
+            return m2, acc
+
+        m, acc = lax.fori_loop(
+            0,
+            jnp.maximum(i, half) + 1,
+            tile,
+            (jnp.full((T, 1), NEG, F32), jnp.zeros((T, 128), F32)),
+        )
+        total = acc[:, 64:65]
+        o = acc / total
+        lse = m + jnp.log(total)
+        R.of[at, :] = jnp.where(lanes(T) < 64, o, lse)
+        for u in range(2):
+            b = i * 2 + u
+            top, bot = o[u * 256 : u * 256 + 128], o[u * 256 + 128 : u * 256 + 256]
+            R.osend[b] = jnp.where(lo2, top, roll64(bot)).astype(BF)
+
+            @pl.when(b != C.dp)
+            def _():
+                C.rc(R.osend.at[b], R.orecv.at[C.dp], k + b, (b, C.t), k + C.dp).start()
+
+    loop(R.Q.shape[0] // T, rows_of)
+    mine = pltpu.make_async_copy(R.osend.at[C.dp], R.orecv.at[C.dp], C.lsem.at[0])
+    mine.start()
+    mine.wait()
+    for b in range(n):
+
+        @pl.when(b != C.dp)
+        def _():
+            cp = C.rc(R.osend.at[b], R.orecv.at[b], k + b, (b, C.t), k + b)
+            cp.wait_send()
+            cp.wait_recv()
+
+    unfold_heads(R.orecv, R.otok, n, seqs)
+
+
+def unfold_heads(src, dst, n, seqs):
+    hp = n // seqs
+    lo2 = lanes(128) < 64
+    for s in range(seqs):
+        for pr in range(hp // 2):
+            e = src[s * hp + 2 * pr].astype(F32)
+            d = src[s * hp + 2 * pr + 1].astype(F32)
+            cut = slice(pr * 128, pr * 128 + 128)
+            dst[s * 256 : s * 256 + 128, cut] = jnp.where(lo2, e, roll64(d)).astype(BF)
+            dst[s * 256 + 128 : s * 256 + 256, cut] = jnp.where(lo2, roll64(e), d).astype(BF)
+
+
+def reduce4(R, C, part, out):
+    k = C.sems(3)
+    k0 = (1 - C.y) * 2 + (1 - C.c)
+    k1 = (1 - C.y) * 2 + C.c
+    k2 = C.y * 2 + (1 - C.c)
+    R.p4[0] = part(k0).astype(BF)
+    c0 = C.send(R.p4.at[0], R.l4.at[0], k, C.mate)
+    v1 = part(k1)
+    c0.wait_recv()
+    R.p4[1] = (v1 + R.l4[0].astype(F32)).astype(BF)
+    c1 = C.send(R.p4.at[1], R.l4.at[2], k + 1, C.yp)
+    R.p4[2] = part(k2).astype(BF)
+    c2 = C.send(R.p4.at[2], R.l4.at[1], k + 2, C.mate)
+    out[...] = part(C.t)
+    c2.wait_recv()
+    c1.wait_recv()
+    out[...] = out[...] + R.l4[1].astype(F32) + R.l4[2].astype(F32)
+
+
+def gather4(R, C, buf):
+    k = C.sems(3)
+    mine = buf.at[C.t]
+    cy = C.send(mine, mine, k, C.yp)
+    cm = C.send(mine, mine, k + 1, C.mate)
+
+    def wait():
+        cy.wait_recv()
+        fwd = C.send(buf.at[C.t_y], buf.at[C.t_y], k + 2, C.mate)
+        cm.wait_recv()
+        fwd.wait_recv()
+
+    return wait
+
+
+def gather8(R, C, buf):
+    k = C.sems(7)
+    mine = buf.at[C.x * 4 + C.t]
+    cd = C.send(mine, mine, k, C.dg)
+    cx = C.send(mine, mine, k + 1, C.xp)
+    cy = C.send(mine, mine, k + 2, C.yp)
+    cm = C.send(mine, mine, k + 3, C.mate)
+
+    def wait():
+        fw = []
+        for i, (cp, slot) in enumerate(
+            (
+                (cy, C.x * 4 + C.t_y),
+                (cx, (1 - C.x) * 4 + C.t),
+                (cd, (1 - C.x) * 4 + C.t_y),
+            )
+        ):
+            cp.wait_recv()
+            fw.append(C.send(buf.at[slot], buf.at[slot], k + 4 + i, C.mate))
+        cm.wait_recv()
+        for cp in fw:
+            cp.wait_recv()
+
+    return wait
+
+
+def stage_out(R, C):
+    def part(k):
+        return mm(R.otok[pl.ds(al(k * CH, CH), CH), :], R.wout[...])
+
+    reduce4(R, C, part, R.x1)
+    rows = R.tok.shape[0]
+    own = pl.ds(al(C.t * CH, CH), CH)
+    pos = C.t * CH + lax.broadcasted_iota(jnp.int32, (CH, rows), 0)
+    col = lax.broadcasted_iota(jnp.int32, (CH, rows), 1)
+    hot = jnp.where(
+        R.routes[...] == lax.broadcasted_iota(jnp.int32, (8, rows), 0), 1.0, 0.0
+    ).astype(BF)
+    earlier = mm_bt(jnp.where(col < pos, 1.0, 0.0).astype(BF), hot)
+    here = mm_bt(jnp.where(col == pos, 1.0, 0.0).astype(BF), hot)
+    keep = jnp.where(earlier < CAP, here, 0.0)
+    keep0, keep1 = keep[:, 0:1], keep[:, 1:2]
+    x1 = R.x1[...] + R.tok[own, :].astype(F32) + R.par[2:3, :]
+    R.x1[...] = x1
+    n, r = norm_parts(x1)
+    h2 = (n * R.par[3:4, :] + R.par[4:5, :]).astype(BF)
+    slot = C.x * 4 + C.t
+    R.H2[slot] = h2
+    hf = h2.astype(F32)
+    l0 = jnp.sum(hf * R.par[5:6, :], axis=1, keepdims=True)
+    l1 = jnp.sum(hf * R.par[6:7, :], axis=1, keepdims=True)
+    mx = jnp.maximum(l0, l1)
+    e0, e1 = jnp.exp(l0 - mx), jnp.exp(l1 - mx)
+    p0, p1 = e0 / (e0 + e1), e1 / (e0 + e1)
+    gate = here[:, 0:1] * p0 + here[:, 1:2] * p1
+    ln = lanes(CH)
+    R.META[slot] = jnp.where(ln == 0, keep0, jnp.where(ln == 1, keep1, 0.0)).astype(BF)
+    wait_h = gather8(R, C, R.H2)
+    wait_m = gather8(R, C, R.META)
+    gr = (gate * R.cot[own, :].astype(F32)).astype(BF)
+    R.GG[slot] = (gr.astype(F32) * (keep0 + keep1)).astype(BF)
+    wait_g = gather8(R, C, R.GG)
+    cols = jnp.zeros((CH, 128), F32)
+    for i, v in enumerate((p0, p1, here[:, 0:1], here[:, 1:2], gate, keep0, keep1)):
+        cols = jnp.where(ln == i, v, cols)
+    R.cols[...] = cols
+    wait_h()
+    wait_m()
+    wait_g()
+
+
+def gelu_both(h):
+    half = 0.5 * (1.0 + lax.erf(h * 0.7071067811865476))
+    return h * half, half + h * (jnp.exp(-0.5 * h * h) * 0.3989422804014327)
+
+
+def stage_moe(R, C):
+    def tile(i):
+        two = pl.ds(al(2 * i, 2), 2)
+        at = pl.ds(al(i * 256, 256), 256)
+        h2 = R.H2[two].reshape(256, R.H2.shape[2])
+        gg = R.GG[two].reshape(256, R.GG.shape[2])
+        meta = R.META[two].reshape(256, 128).astype(F32)
+        m0, m1 = meta[:, 0:1], meta[:, 1:2]
+        half = R.wi.shape[2]
+        bias0 = R.inb[0:1, pl.ds(al(C.x * half, half), half)].astype(F32)
+        bias1 = R.inb[1:2, pl.ds(al(C.x * half, half), half)].astype(F32)
+        for q in range(half // 256):
+            cut = slice(q * 256, q * 256 + 256)
+            h0 = mm(h2, R.wi[0, :, cut]) + bias0[:, cut]
+            h1 = mm(h2, R.wi[1, :, cut]) + bias1[:, cut]
+            act, slope = gelu_both(jnp.where(m0 > 0.0, h0, h1))
+            R.A[0, at, cut] = (act * m0).astype(BF)
+            R.A[1, at, cut] = (act * m1).astype(BF)
+            d0 = mm_bt(gg, R.wb[0, cut, :])
+            d1 = mm_bt(gg, R.wb[1, cut, :])
+            dh = jnp.where(m0 > 0.0, d0, d1) * slope
+            R.DH[0, at, cut] = (dh * m0).astype(BF)
+            R.DH[1, at, cut] = (dh * m1).astype(BF)
+        y = mm(R.A[0, at, :], R.wb[0]) + mm(R.A[1, at, :], R.wb[1])
+        R.YP[two] = y.astype(BF).reshape(2, CH, y.shape[1])
+        dx = mm_bt(R.DH[0, at, :], R.wi[0]) + mm_bt(R.DH[1, at, :], R.wi[1])
+        R.DXP[two] = dx.astype(BF).reshape(2, CH, dx.shape[1])
+
+    loop(4, tile)
+
+
+def stage_moe_grads(R, C):
+    rows = R.GG.shape[0] * CH
+
+    def back(i):
+        at = pl.ds(al(i * 128, 128), 128)
+        gg = R.GG[...].reshape(rows, R.GG.shape[2])
+        for e in range(2):
+            R.gB[e, at, :] = mm_at(R.A[e, :, at], gg).astype(BF)
+
+    loop(R.A.shape[2] // 128, back)
+
+    def into(i):
+        at = pl.ds(al(i * 128, 128), 128)
+        h2t = R.H2[:, :, at].reshape(rows, 128)
+        for e in range(2):
+            R.gI[e, at, :] = mm_at(h2t, R.DH[e]).astype(BF)
+
+    loop(R.gI.shape[1] // 128, into)
+
+
+def reduce8(R, C, parts, land, stage, out):
+    k = C.sems(7)
+    order = ((1 - C.x, 1 - C.y), (1 - C.x, C.y), (C.x, 1 - C.y), (C.x, C.y))
+    devs = (C.dg, C.xp, C.yp)
+    cm = []
+    for n, (xx, yy) in enumerate(order):
+        cm.append(C.send(parts.at[xx * 4 + yy * 2 + 1 - C.c], land.at[n], k + n, C.mate))
+    cr = []
+    for n, (xx, yy) in enumerate(order):
+        cm[n].wait_recv()
+        v = parts[xx * 4 + yy * 2 + C.c].astype(F32) + land[n].astype(F32)
+        if n < 3:
+            stage[n] = v.astype(BF)
+            cr.append(C.send(stage.at[n], land.at[4 + n], k + 4 + n, devs[n]))
+        else:
+            out[...] = v
+
+    def wait():
+        for n in range(3):
+            cr[n].wait_recv()
+        out[...] = (
+            out[...] + land[4].astype(F32) + land[5].astype(F32) + land[6].astype(F32)
+        )
+
+    return wait
+
+
+def norm_back(n, r, dn):
+    return r * (
+        dn - jnp.mean(dn, axis=-1, keepdims=True) - n * jnp.mean(dn * n, axis=-1, keepdims=True)
+    )
+
+
+def rowsum(v):
+    return jnp.sum(v, axis=0, keepdims=True)
+
+
+def stage_owner(R, C):
+    own = pl.ds(al(C.t * CH, CH), CH)
+    cols = R.cols[...]
+    p0, p1, h0, h1, gate, k0, k1 = (cols[:, i : i + 1] for i in range(7))
+    u = R.u[...] + k0 * R.par[7:8, :] + k1 * R.par[8:9, :]
+    g = R.cot[own, :].astype(F32)
+    x1 = R.x1[...]
+    R.RES[C.t] = (x1 + gate * u).astype(BF)
+    dg = jnp.sum(g * u, axis=1, keepdims=True) * gate
+    dl0 = (dg * (h0 - p0)).astype(BF).astype(F32)
+    dl1 = (dg * (h1 - p1)).astype(BF).astype(F32)
+    h2 = R.H2[C.x * 4 + C.t].astype(F32)
+    gg = R.GG[C.x * 4 + C.t].astype(F32)
+    dh2 = R.dx[...] + dl0 * R.par[5:6, :] + dl1 * R.par[6:7, :]
+    n, r = norm_parts(x1)
+    dx1 = g + norm_back(n, r, dh2 * R.par[3:4, :])
+    da = dx1.astype(BF)
+    R.DA[C.t] = da
+    R.x1[...] = dx1
+    R.sm[0:1, :] = rowsum(dh2 * n)
+    R.sm[1:2, :] = rowsum(dh2)
+    R.sm[2:3, :] = rowsum(da.astype(F32))
+    R.sm[3:4, :] = rowsum(h2 * dl0)
+    R.sm[4:5, :] = rowsum(h2 * dl1)
+    R.sm[5:6, :] = rowsum(gg * k0)
+    R.sm[6:7, :] = rowsum(gg * k1)
+
+
+def stage_out_back(R, C, n):
+    seqs = R.prefix.shape[0]
+    hp = n // seqs
+    lo2 = lanes(128) < 64
+    for s in range(seqs):
+        da = R.DA[2 * s : 2 * s + 2].reshape(256, R.DA.shape[2])
+        for pr in range(hp // 2):
+            cut = slice(pr * 128, pr * 128 + 128)
+            d = mm_bt(da, R.wout[cut, :])
+            a, b = d[0:128], d[128:256]
+            R.osend[s * hp + 2 * pr] = jnp.where(lo2, a, roll64(b)).astype(BF)
+            R.osend[s * hp + 2 * pr + 1] = jnp.where(lo2, roll64(a), b).astype(BF)
+
+
+def stage_out_grad(R, C):
+    da = R.DA[...].reshape(R.otok.shape[0], R.DA.shape[2])
+    for pr in range(R.otok.shape[1] // 128):
+        cut = slice(pr * 128, pr * 128 + 128)
+        R.gO[cut, :] = mm_at(R.otok[:, cut], da).astype(BF)
+
+
+def stage_attend_back(R, C, n):
+    lo2 = lanes(128) < 64
+    ln2 = lanes(128)
+
+    def hi_lo(v):
+        hi = v.astype(BF).astype(F32)
+        return hi, v - hi
+
+    def unpack(b):
+        f = R.dorecv[b].astype(F32)
+        for u in range(2):
+            at = pl.ds(al(b * 256 + u * 128, 128), 128)
+            do = jnp.where(lo2, f if u == 0 else roll64(f), 0.0)
+            of = R.of[at, :]
+            hi, low = hi_lo(-jnp.sum(do * of, axis=1, keepdims=True))
+            R.DO[at, :] = jnp.where(ln2 == 64, hi, jnp.where(ln2 == 65, low, do)).astype(BF)
+            hi, low = hi_lo(-of[:, 64:65])
+            q = R.Q[at, :].astype(F32)
+            R.Q[at, :] = jnp.where(ln2 == 64, hi, jnp.where(ln2 == 65, low, q)).astype(BF)
+
+    loop(n, unpack)
+    T = 512
+    total = R.Q.shape[0]
+    nt = total // T
+    half = nt // 2
+    seqs = R.prefix.shape[0]
+    prefix = R.prefix[C.dp // (n // seqs)]
+    R.dq[...] = jnp.zeros_like(R.dq)
+    k = C.sems(n)
+    k2 = C.sems(n)
+
+    def keys(jj):
+        j = nt - 1 - jj
+        kat = pl.ds(al(j * T, T), T)
+        kk, vv = R.K[kat, :], R.V[kat, :]
+        kpos = j * T + lax.broadcasted_iota(jnp.int32, (T, T), 0)
+
+        def tile(i, carry):
+            dk, dv = carry
+            qat = pl.ds(al(i * T, T), T)
+            q, do = R.Q[qat, :], R.DO[qat, :]
+            qpos = i * T + lax.broadcasted_iota(jnp.int32, (1, T), 1)
+            lim = jnp.maximum(qpos, prefix - 1)
+            p = jnp.where(kpos <= lim, jnp.exp(mm_bt(kk, q)), 0.0)
+            ds = (p * mm_bt(vv, do)).astype(BF)
+            dv = dv + mm(p.astype(BF), do)
+            dk = dk + mm(ds, q)
+            R.dq[qat, :] = R.dq[qat, :] + mm_at(ds, kk)
+            return dk, dv
+
+        first = jnp.where(j >= half, j, 0)
+        dk, dv = lax.fori_loop(
+            first, nt, tile, (jnp.zeros((T, 128), F32), jnp.zeros((T, 128), F32))
+        )
+        lo = lanes(T) < 64
+        kv = jnp.where(lo, dk, roll64(dv)).astype(BF)
+        for u in range(2):
+            b = j * 2 + u
+            R.kvs[b] = kv[u * 256 : u * 256 + 256]
+
+            @pl.when(b != C.dp)
+            def _():
+                C.rc(R.kvs.at[b], R.kvr.at[C.dp], k + b, (b, C.t), k + C.dp).start()
+
+    loop(nt, keys)
+
+    def queries(b):
+        at = al(b * 256, 256)
+        top = R.dq[pl.ds(at, 128), :] * 0.125
+        bot = R.dq[pl.ds(al(at + 128, 128), 128), :] * 0.125
+        R.osend[b] = jnp.where(lo2, top, roll64(bot)).astype(BF)
+
+        @pl.when(b != C.dp)
+        def _():
+            C.rc(R.osend.at[b], R.dqrecv.at[C.dp], k2 + b, (b, C.t), k2 + C.dp).start()
+
+    loop(n, queries)
+    for src, dst, i in ((R.osend, R.dqrecv, 0), (R.kvs, R.kvr, 1)):
+        mine = pltpu.make_async_copy(src.at[C.dp], dst.at[C.dp], C.lsem.at[i])
+        mine.start()
+        mine.wait()
+    for src, dst, kk in ((R.kvs, R.kvr, k), (R.osend, R.dqrecv, k2)):
+        for b in range(n):
+
+            @pl.when(b != C.dp)
+            def _():
+                cp = C.rc(src.at[b], dst.at[b], kk + b, (b, C.t), kk + b)
+                cp.wait_send()
+                cp.wait_recv()
+
+    hp = n // seqs
+    lo = lanes(256) < 64
+    for s in range(seqs):
+        for pr in range(hp // 2):
+            p = s * hp + 2 * pr
+            cut = slice(pr * 128, pr * 128 + 128)
+            e, d = R.kvr[p].astype(F32), R.kvr[p + 1].astype(F32)
+            R.dproj[1, s * 256 : s * 256 + 256, cut] = jnp.where(lo, e, roll64(d)).astype(BF)
+            R.dproj[2, s * 256 : s * 256 + 256, cut] = jnp.where(lo, roll64(e), d).astype(BF)
+    unfold_heads(R.dqrecv, R.dproj.at[0], n, seqs)
+
+
+def stage_qkv_back(R, C):
+    def part(k):
+        at = pl.ds(al(k * CH, CH), CH)
+        return (
+            mm_bt(R.dproj[0, at, :], R.wqkv[0])
+            + mm_bt(R.dproj[1, at, :], R.wqkv[1])
+            + mm_bt(R.dproj[2, at, :], R.wqkv[2])
+        )
+
+    reduce4(R, C, part, R.dx)
+    own = pl.ds(al(C.t * CH, CH), CH)
+    n, r = norm_parts(R.tok[own, :].astype(F32))
+    dh1 = R.dx[...]
+    R.GIN[C.t] = (R.x1[...] + norm_back(n, r, dh1 * R.par[0:1, :])).astype(BF)
+    R.sm2[0:1, :] = rowsum(dh1 * n)
+    R.sm2[1:2, :] = rowsum(dh1)
+
+
+def stage_qkv_grad(R, C):
+    def cols(i):
+        at = pl.ds(al(i * 128, 128), 128)
+        h = R.h1[:, at]
+        for m in range(3):
+            R.gQ[m, at, :] = mm_at(h, R.dproj[m]).astype(BF)
+
+    loop(R.h1.shape[1] // 128, cols)
+
+
+class Line:
+    def __init__(self, C, nz, n, src, land, out, locals_at):
+        self.C, self.nz, self.n = C, nz, n
+        self.src, self.land, self.out = src, land, out
+        self.red, self.bc, self.xs = C.sems(2 * n), C.sems(2 * n), C.sems(2 * n)
+        self.loc = locals_at
+
+    def place(self, d):
+        C = self.C
+        step = 1 if d == 0 else -1
+        pos = C.z if d == 0 else self.nz - 1 - C.z
+        up = (C.dp + 2 * step, C.t)
+        down = (C.dp - 2 * step, C.t)
+        return pos, up, down
+
+    def copies(self, d, k):
+        C = self.C
+        pos, up, down = self.place(d)
+        i = d * self.n + k
+        mine = self.out(C.x, d, k)
+        return pos, dict(
+            red=lambda: C.rc(self.src(d, k), self.land(d, k), self.red + i, up),
+            bc_src=lambda: C.rc(self.src(d, k), mine, self.bc + i, down),
+            bc_out=lambda: C.rc(mine, mine, self.bc + i, down),
+            xs_src=lambda: C.rc(self.src(d, k), mine, self.xs + i, C.xp),
+            xs_out=lambda: C.rc(mine, mine, self.xs + i, C.xp),
+            xs_in=lambda: C.rc(self.out(1 - C.x, d, k), self.out(1 - C.x, d, k), self.xs + i, C.xp),
+            keep=lambda: pltpu.make_async_copy(self.src(d, k), mine, C.lsem.at[self.loc + i]),
+        )
+
+    def reduce(self, d, k):
+        pos, c = self.copies(d, k)
+
+        @pl.when(pos > 0)
+        def _():
+            c["red"]().wait_recv()
+            s, l = self.src(d, k), self.land(d, k)
+            rows = s.shape[0]
+
+            def add(i):
+                at = pl.ds(al(i * 16, 16), 16)
+                s[at, :] = (s[at, :].astype(F32) + l[at, :].astype(F32)).astype(BF)
+
+            loop(rows // 16, add)
+
+        @pl.when(pos < self.nz - 1)
+        def _():
+            c["red"]().start()
+
+        @pl.when(pos == self.nz - 1)
+        def _():
+            c["bc_src"]().start()
+            c["xs_src"]().start()
+            c["keep"]().start()
+
+    def spread(self, d, k):
+        pos, c = self.copies(d, k)
+
+        @pl.when(pos < self.nz - 1)
+        def _():
+            c["bc_out"]().wait_recv()
+
+            @pl.when(pos > 0)
+            def _():
+                c["bc_out"]().start()
+
+            c["xs_out"]().start()
+
+    def finish(self):
+        def one(k):
+            for d in range(2):
+                pos, c = self.copies(d, k)
+                c["xs_in"]().wait_recv()
+                c["xs_out"]().wait_send()
+
+                @pl.when(pos < self.nz - 1)
+                def _():
+                    c["red"]().wait_send()
+
+                @pl.when(pos > 0)
+                def _():
+                    c["bc_out"]().wait_send()
+
+                @pl.when(pos == self.nz - 1)
+                def _():
+                    c["keep"]().wait()
+
+        loop(self.n, one)
+
+
+def exchange_x(C, full, land, half):
+    k = C.sems(1)
+    lead = (slice(None),) * (len(full.shape) - 2)
+    theirs = pl.ds(al((1 - C.x) * half, half), half)
+    cp = C.send(full.at[lead + (theirs,)], land, k, C.xp)
+
+    def wait():
+        cp.wait_recv()
+        groups = full.shape[0] if lead else 1
+        for m in range(groups):
+
+            def add(i):
+                at = pl.ds(al(i * 16, 16), 16)
+                own = pl.ds(al(C.x * half + i * 16, 16), 16)
+                if lead:
+                    v = full[m, own, :].astype(F32) + land[m, at, :].astype(F32)
+                    full[m, own, :] = v.astype(BF)
+                else:
+                    v = full[own, :].astype(F32) + land[at, :].astype(F32)
+                    full[own, :] = v.astype(BF)
+
+            loop(half // 16, add)
+
+    return wait
+
+
+def stage_small(R, C, n):
+    R.st[C.t, 0:8, :] = R.sm[...]
+    R.st[C.t, 8:16, :] = R.sm2[...]
+    k = C.sems(3)
+    cps = [
+        C.send(R.st.at[C.t], R.st.at[C.t], k + i, dev)
+        for i, dev in enumerate((C.mate, C.yp, (C.dp, 3 - C.t)))
+    ]
+    for cp in cps:
+        cp.wait_recv()
+    tot = R.st[0] + R.st[1] + R.st[2] + R.st[3]
+    sd = R.sd.at[C.dp]
+    sd[0:8, :] = tot[0:8, :]
+    sd[8:10, :] = tot[8:10, :]
+    f = R.dproj.shape[2]
+
+    def colsum(m):
+        return rowsum(R.dproj[m].astype(F32))
+
+    sd[10:11, 0:f] = colsum(0)
+    sd[10:11, f : 2 * f] = colsum(2)
+    half = R.DH.shape[2]
+    for e in range(2):
+        sd[11:12, e * half : (e + 1) * half] = rowsum(R.DH[e].astype(F32))
+    k = C.sems(n)
+    cps = [
+        C.send(sd, R.sd.at[C.dp], k + o, (lax.rem(C.dp + o, n), C.t)) for o in range(1, n)
+    ]
+    for cp in cps:
+        cp.wait_recv()
+    tot = R.sd[0]
+    for b in range(1, n):
+        tot = tot + R.sd[b]
+    R.osm[...] = tot
+    for xx in range(2):
+        v = R.sd[xx, 11:12, :]
+        for b in range(2 + xx, n, 2):
+            v = v + R.sd[b, 11:12, :]
+        R.osm[11 + xx : 12 + xx, :] = v
+
+
+class Refs:
+    pass
+
+
+ROWS_B, ROWS_I = 64, 128
+
+
+def body(names, n, nz, *refs):
+    R = Refs()
+    for name, ref in zip(names, refs):
+        setattr(R, name, ref)
+    C = Ctx(R.ssem, R.rsem, R.lsem)
+    sem, count = barrier_start(C, n)
+    half = R.wi.shape[2]
+    off = pl.ds(al(C.x * half, half), half)
+    wcp = [
+        pltpu.make_async_copy(R.w_in.at[:, :, off], R.wi, C.lsem.at[2]),
+        pltpu.make_async_copy(R.w_back.at[:, off, :], R.wb, C.lsem.at[3]),
+    ]
+    for cp in wcp:
+        cp.start()
+    R.sm[...] = jnp.zeros_like(R.sm)
+    R.sm2[...] = jnp.zeros_like(R.sm2)
+    R.sd[...] = jnp.zeros_like(R.sd)
+    stage_qkv(R, C)
+    pl.semaphore_wait(sem, count)
+    all_to_all(R, C, R.asend, R.arecv, n)()
+    stage_attend(R, C, n)
+    stage_out(R, C)
+    for cp in wcp:
+        cp.wait()
+    stage_moe(R, C)
+    wait_u = reduce8(R, C, R.YP, R.ly, R.sy, R.u)
+    wait_x = reduce8(R, C, R.DXP, R.lx, R.sx, R.dx)
+    stage_moe_grads(R, C)
+
+    lb = Line(
+        C, nz, half // ROWS_B,
+        lambda d, k: R.gB.at[d, pl.ds(al(k * ROWS_B, ROWS_B), ROWS_B), :],
+        lambda d, k: R.lB.at[d, pl.ds(al(k * ROWS_B, ROWS_B), ROWS_B), :],
+        lambda h, d, k: R.oB.at[d, pl.ds(al(h * half + k * ROWS_B, ROWS_B), ROWS_B), :],
+        4,
+    )
+    D = R.gI.shape[1]
+    li = Line(
+        C, nz, D // ROWS_I,
+        lambda d, k: R.gI.at[d, pl.ds(al(k * ROWS_I, ROWS_I), ROWS_I), :],
+        lambda d, k: R.lI.at[d, pl.ds(al(k * ROWS_I, ROWS_I), ROWS_I), :],
+        lambda h, d, k: R.oI.at[
+            d, pl.ds(al(k * ROWS_I, ROWS_I), ROWS_I), pl.ds(al(h * half, half), half)
+        ],
+        4 + 2 * lb.n,
+    )
+
+    wait_u()
+    wait_x()
+    stage_owner(R, C)
+    wait_da = gather4(R, C, R.DA)
+    wait_res = gather4(R, C, R.RES)
+    wait_da()
+    stage_out_back(R, C, n)
+    wait_do = all_to_all(R, C, R.osend, R.dorecv, n)
+    stage_out_grad(R, C)
+    wait_do()
+    C.drain()
+    stage_attend_back(R, C, n)
+    stage_qkv_back(R, C)
+    wait_gin = gather4(R, C, R.GIN)
+    stage_qkv_grad(R, C)
+    F = R.gO.shape[0]
+    hq, ho = D // 2, F // 2
+    wq = exchange_x(C, R.gQ, R.xQ, hq)
+    wo = exchange_x(C, R.gO, R.xO, ho)
+    wq()
+    wo()
+    wait_gin()
+    wait_res()
+    qd, od = hq // 2, ho // 2
+    lq = Line(
+        C, nz, 3,
+        lambda d, k: R.gQ.at[k, pl.ds(al(C.x * hq + d * qd, qd), qd), :],
+        lambda d, k: R.lQ.at[d, k],
+        lambda h, d, k: R.oQ.at[k, pl.ds(al(h * hq + d * qd, qd), qd), :],
+        4 + 2 * lb.n + 2 * li.n,
+    )
+    lo = Line(
+        C, nz, 1,
+        lambda d, k: R.gO.at[pl.ds(al(C.x * ho + d * od, od), od), :],
+        lambda d, k: R.lO.at[d],
+        lambda h, d, k: R.oO.at[pl.ds(al(h * ho + d * od, od), od), :],
+        4 + 2 * lb.n + 2 * li.n + 6,
+    )
+    work = [(L, k) for L in (lb, li, lq, lo) for k in range(L.n)]
+    lag = 4
+    for s in range(len(work) + lag):
+        if s < len(work):
+            L, k = work[s]
+            L.reduce(0, k)
+            L.reduce(1, k)
+        if s >= lag:
+            L, k = work[s - lag]
+            L.spread(0, k)
+            L.spread(1, k)
+    stage_small(R, C, n)
+    for L in (lb, li, lq, lo):
+        L.finish()
+    C.drain()
+
+
+def fast_local(args, n, nt):
+    (tokens, g1, b1, w_qkv, qvb, w_out, out_b, g2, b2, router, w_in, in_b, w_back, back_b,
+     routes, prefix, cot) = args
+    S, span, D = tokens.shape
+    rows = S * span
+    F = w_qkv.shape[2]
+    H = w_in.shape[2]
+    half = H // 2
+    nz = n // 2
+    total = n * span
+    par = jnp.concatenate(
+        [jnp.stack([g1, b1, out_b, g2, b2]), router.T, back_b, jnp.zeros((7, D), BF)], axis=0
+    ).astype(F32)
+    vm = pl.BlockSpec(memory_space=pltpu.VMEM)
+    hbm = pl.BlockSpec(memory_space=pl.ANY)
+    ins = [
+        ("tok", tokens.reshape(rows, D), vm),
+        ("par", par, vm),
+        ("wqkv", w_qkv.transpose(1, 0, 2), vm),
+        ("qvb", qvb, vm),
+        ("wout", w_out, vm),
+        ("routes", routes.reshape(1, rows), vm),
+        ("prefix", prefix, pl.BlockSpec(memory_space=pltpu.SMEM)),
+        ("cot", cot.reshape(rows, D), vm),
+        ("inb", in_b, vm),
+        ("w_in", w_in, hbm),
+        ("w_back", w_back, hbm),
+    ]
+    sds = jax.ShapeDtypeStruct
+    outs = [
+        ("RES", sds((nt, CH, D), BF), vm),
+        ("GIN", sds((nt, CH, D), BF), vm),
+        ("oB", sds((2, H, D), BF), hbm),
+        ("oI", sds((2, D, H), BF), hbm),
+        ("oQ", sds((3, D, F), BF), hbm),
+        ("oO", sds((F, D), BF), hbm),
+        ("osm", sds((16, D), F32), vm),
+    ]
+    V = pltpu.VMEM
+    nch = half // ROWS_B + D // ROWS_I + 4
+    scr = [
+        ("h1", V((rows, D), BF)),
+        ("asend", V((n, 384, 128), BF)),
+        ("arecv", V((n, 384, 128), BF)),
+        ("Q", V((total, 128), BF)),
+        ("K", V((total, 128), BF)),
+        ("V", V((total, 128), BF)),
+        ("DO", V((total, 128), BF)),
+        ("of", V((total, 128), F32)),
+        ("dq", V((total, 128), F32)),
+        ("osend", V((n, 128, 128), BF)),
+        ("orecv", V((n, 128, 128), BF)),
+        ("dorecv", V((n, 128, 128), BF)),
+        ("dqrecv", V((n, 128, 128), BF)),
+        ("kvs", V((n, 256, 128), BF)),
+        ("kvr", V((n, 256, 128), BF)),
+        ("otok", V((rows, F), BF)),
+        ("dproj", V((3, rows, F), BF)),
+        ("p4", V((3, CH, D), BF)),
+        ("l4", V((3, CH, D), BF)),
+        ("x1", V((CH, D), F32)),
+        ("u", V((CH, D), F32)),
+        ("dx", V((CH, D), F32)),
+        ("cols", V((CH, 128), F32)),
+        ("H2", V((8, CH, D), BF)),
+        ("GG", V((8, CH, D), BF)),
+        ("META", V((8, CH, 128), BF)),
+        ("wi", V((2, D, half), BF)),
+        ("wb", V((2, half, D), BF)),
+        ("A", V((2, 8 * CH, half), BF)),
+        ("DH", V((2, 8 * CH, half), BF)),
+        ("YP", V((8, CH, D), BF)),
+        ("DXP", V((8, CH, D), BF)),
+        ("ly", V((7, CH, D), BF)),
+        ("lx", V((7, CH, D), BF)),
+        ("sy", V((3, CH, D), BF)),
+        ("sx", V((3, CH, D), BF)),
+        ("DA", V((nt, CH, D), BF)),
+        ("gB", V((2, half, D), BF)),
+        ("gI", V((2, D, half), BF)),
+        ("gQ", V((3, D, F), BF)),
+        ("gO", V((F, D), BF)),
+        ("lB", V((2, half, D), BF)),
+        ("lI", V((2, D, half), BF)),
+        ("xQ", V((3, D // 2, F), BF)),
+        ("xO", V((F // 2, D), BF)),
+        ("lQ", V((2, 3, D // 4, F), BF)),
+        ("lO", V((2, F // 4, D), BF)),
+        ("sm", V((8, D), F32)),
+        ("sm2", V((8, D), F32)),
+        ("st", V((4, 16, D), F32)),
+        ("sd", V((n, 16, D), F32)),
+        ("ssem", pltpu.SemaphoreType.DMA((120 + 6 * nch,))),
+        ("rsem", pltpu.SemaphoreType.DMA((120 + 6 * nch,))),
+        ("lsem", pltpu.SemaphoreType.DMA((8 + 2 * nch,))),
+    ]
+    names = [i[0] for i in ins] + [o[0] for o in outs] + [s[0] for s in scr]
+    res, gin, oB, oI, oQ, oO, osm = pl.pallas_call(
+        functools.partial(body, names, n, nz),
+        out_shape=[o[1] for o in outs],
+        in_specs=[i[2] for i in ins],
+        out_specs=[o[2] for o in outs],
+        scratch_shapes=[s[1] for s in scr],
+        compiler_params=pltpu.CompilerParams(
+            collective_id=0, has_side_effects=True, vmem_limit_bytes=67043328
+        ),
+        name="layer",
+    )(*[i[1] for i in ins])
+    inb = jnp.stack([osm[11].reshape(2, half), osm[12].reshape(2, half)], axis=1).reshape(2, H)
+    return (
+        res.reshape(S, span, D).astype(F32),
+        gin.reshape(S, span, D).astype(F32),
+        osm[8],
+        osm[9],
+        oQ.astype(F32).transpose(1, 0, 2),
+        osm[10, : 2 * F].reshape(2, F),
+        oO.astype(F32),
+        osm[2],
+        osm[0],
+        osm[1],
+        osm[3:5].T,
+        oI.astype(F32),
+        inb,
+        oB.astype(F32),
+        osm[5:7],
+    )
 
 
 SCALE = 0.125
@@ -95,7 +1104,7 @@
         is_live = block_live(key_start, query_last, prefix)
         return (
             lax.cond(
-                is_live, partial(attend_update, block_index), lambda unchanged: unchanged, state_now
+                is_live, functools.partial(attend_update, block_index), lambda unchanged: unchanged, state_now
             ),
             None,
         )
@@ -189,7 +1198,7 @@
         is_live = block_live(first_row, query_last, prefix)
         return (
             lax.cond(
-                is_live, partial(query_update, block_index), lambda unchanged: unchanged, state_now
+                is_live, functools.partial(query_update, block_index), lambda unchanged: unchanged, state_now
             ),
             None,
         )
@@ -243,7 +1252,7 @@
         jnp.zeros(stat_shape, jnp.float32),
         jnp.zeros(queries.shape, jnp.float32),
     )
-    fold_keys = partial(attend_fold, queries=queries, first_row=first_row, prefix=prefix)
+    fold_keys = functools.partial(attend_fold, queries=queries, first_row=first_row, prefix=prefix)
     run_max, run_sum, run_out = fold_keys(
         start_state,
         (
@@ -289,7 +1298,7 @@
         jnp.einsum("ecd,edf->ecf", dispatched, w_in, preferred_element_type=jnp.float32)
         + in_bias.astype(jnp.float32)[:, None, :]
     )
-    act_float, gelu_pull = jax.vjp(partial(jax.nn.gelu, approximate=False), pre_act)
+    act_float, gelu_pull = jax.vjp(functools.partial(jax.nn.gelu, approximate=False), pre_act)
     active = act_float.astype(jnp.bfloat16)
     expert_part = jnp.einsum("ecf,efd->ecd", active, w_back, preferred_element_type=jnp.float32)
     expert_full = lax.psum(expert_part, "tensor") + back_bias.astype(jnp.float32)[:, None, :]
@@ -335,7 +1344,7 @@
     )
     total_rows = log_total.transpose(0, 2, 1)
     delta_rows = delta.transpose(0, 2, 1)
-    fold_rows = partial(
+    fold_rows = functools.partial(
         query_fold,
         key_heads=heads_of(key_tok, head_count),
         value_heads=heads_of(value_tok, head_count),
@@ -430,4 +1439,18 @@
         P(None, "tensor", None),
         P(),
     )
-    return jax.shard_map(local, mesh=mesh, in_specs=in_specs, out_specs=out_specs, check_vma=False)
+    n, nt = mesh.shape["dp"], mesh.shape["tensor"]
+
+    def step(*args):
+        tokens, w_qkv = args[0], args[3]
+        heads = w_qkv.shape[2] // HEAD_DIM
+        fits = (
+            nt == 4
+            and n % 2 == 0
+            and n == tokens.shape[0] * heads
+            and tokens.shape[0] * tokens.shape[1] == nt * CH
+            and tokens.shape[1] == 256
+        )
+        return fast_local(args, n, nt) if fits else local(*args)
+
+    return jax.shard_map(step, mesh=mesh, in_specs=in_specs, out_specs=out_specs, check_vma=False)

time: 1300 us -> 857 us (0.66)
  waiting for transfers between devices: 886 us -> 0 us
  Pallas kernels: 0 us -> 824 us
  matrix products: 140 us -> 0 us
  blocking collectives: 86.8 us -> 0 us
  local copies, waits for them, and re-layouts: 86.2 us -> 9.32 us
  other arithmetic: 54.7 us -> 19.5 us
  loops' own time: 20.3 us -> 0 us
  between operations: 15 us -> 0.67 us
    pallas_call x0 -> x1, Pallas kernels: none -> 824 us  [fast_local(): pl.pallas_call(functools.partial(body, names, n, nz), out_shape=[o[1] for...]
    psum x5 -> x0, waiting for transfers between devices: 793 us -> none  [the longest x1 584 us: local(): lax.psum((grad_ln1_gain, grad_ln1_bias, grad_w_qkv, grad_qv_bias, grad_w_...]
    dot_general x39 -> x0, matrix products: 140 us -> none  [the longest x4 24.1 us: query_update(): jnp.einsum('shqk,shqd->shkd', probs, douts.astype(jnp.float32), precision...]
    all_gather x4 -> x0, waiting for transfers between devices: 93.5 us -> none  [the longest x1 51.2 us: local(): lax.all_gather(value_tok, 'dp', axis=1, tiled=True)]
    all_gather x2 -> x0, blocking collectives: 46.3 us -> none  [the longest x1 26.4 us: local(): lax.all_gather(total_rows.astype(jnp.bfloat16), 'dp', axis=1, tiled=True)]
    psum x1 -> x0, blocking collectives: 40.5 us -> none  [local(): lax.psum((grad_ln1_gain, grad_ln1_bias, grad_w_qkv, grad_qv_bias, grad_w_...]
    unnamed x121 -> x6, local copies, waits for them, and re-layouts: 27.5 us -> 0.01 us
    dynamic_slice x20 -> x0, local copies, waits for them, and re-layouts: 25.8 us -> none  [the longest x12 9.72 us: attend_fold(): lax.scan(attend_block_step, run_state, jnp.arange(row_count // block_widt...]
  transfers between devices with their start and end apart: 9 -> 0, of which waited for: 7 -> 0; matrix products, arithmetic and copies ran while one was open for 8% -> 0% of each run, Pallas kernels for 0% -> 0%
where the time goes in v1:
time: 857 us; the launch traced here: 854 us
  Pallas kernels  824 us (96%)
  other arithmetic  19.5 us (2%)
  local copies, waits for them, and re-layouts  9.32 us (1%)
    pallas_call x1, Pallas kernels, fast_local(): pl.pallas_call(functools.partial(body, names, n, nz), out_shape=[o[1] for...  824 us

profile of v1, /device:TPU:0, one launch (start us, length us, event | category | flops | bytes accessed | tf_op | source)
XLA Modules:
  0.0 853.5 jit_solution(259620658164653414)
XLA Ops:
  0.6 0.7 stack.18
  1.3 0.7 stack.19
  2.0 0.7 stack.20
  2.7 0.7 stack.21
  3.4 0.7 stack.22
  4.1 1.6 concatenate.3
  5.6 0.6 convert_element_type.25.refs_1_
  6.3 824.0 %layer.1 = (bf16[4,128,1024]{2,1,0:T(8,128)(2,1)}, bf16[4,128,1024]{2,1,0:T(8,128)(2,1)}, bf16[2,1024,1024]{2,1,0:T(8,128)(2,1)}, bf16[2,1024,1024]{2,1,0:T(8,12...) custom-call(bf16[512,1024]{1,0:T(8,128)(2,1)} %bitcast.25, ...), custom_call_target="tpu_custom_call" | custom-call | tf_op jit(solution)/shard_map/layer/pallas_call | solution.py:991
  830.3 1.5 slice_reduce_fusion.1
  831.9 0.6 pad_maximum_fusion
  832.5 4.0 bitcast_convert_fusion
  836.5 1.4 fusion
  837.9 0.7 slice_reduce_fusion.2
  838.7 0.6 reshape_squeeze.3
  839.3 0.0 copy-start
  839.3 6.8 convert_element_type.31
  846.1 0.0 copy-done
  846.1 0.0 copy-start.1
  846.1 4.4 convert_element_type.32
  850.5 0.0 copy-start.2
  850.5 0.0 copy-done.1
  850.5 1.9 convert_bitcast_fusion
  852.4 0.0 copy-done.2
  852.4 1.1 convert_element_type.30
  (3 shorter events, 0.0 us)
Async XLA Ops:
  839.3 6.8 copy-start
  846.1 4.4 copy-start.1
  850.5 1.9 copy-start.2

commit v2 on v1

--- a/solution.py
+++ b/solution.py
@@ -389,24 +389,37 @@
     loop(4, tile)
 
 
-def stage_moe_grads(R, C):
+def put_wide(at, v):
+    w = v.shape[1] // 2
+    at[0:32, :] = v[:, 0:w].astype(BF)
+    at[32:64, :] = v[:, w : 2 * w].astype(BF)
+
+
+def stage_moe_grads(R, C, K, ring):
     rows = R.GG.shape[0] * CH
 
     def back(i):
         at = pl.ds(al(i * 128, 128), 128)
         gg = R.GG[...].reshape(rows, R.GG.shape[2])
         for e in range(2):
-            R.gB[e, at, :] = mm_at(R.A[e, :, at], gg).astype(BF)
+            v = mm_at(R.A[e, :, at], gg)
+            for j in range(4):
+                put_wide(R.G.at[e, 4 * i + j], v[32 * j : 32 * j + 32])
 
     loop(R.A.shape[2] // 128, back)
+    ring.run(3)
+    base = ring.take(R.H2.shape[2] // 128)
 
     def into(i):
         at = pl.ds(al(i * 128, 128), 128)
         h2t = R.H2[:, :, at].reshape(rows, 128)
         for e in range(2):
-            R.gI[e, at, :] = mm_at(h2t, R.DH[e]).astype(BF)
-
-    loop(R.gI.shape[1] // 128, into)
+            v = mm_at(h2t, R.DH[e]).astype(BF)
+            R.G[e, K.i0 + 2 * i] = v[0:64]
+            R.G[e, K.i0 + 2 * i + 1] = v[64:128]
+        ring.tick(base + i)
+
+    loop(R.H2.shape[2] // 128, into)
 
 
 def reduce8(R, C, parts, land, stage, out):
@@ -488,14 +501,34 @@
             R.osend[s * hp + 2 * pr + 1] = jnp.where(lo2, roll64(a), b).astype(BF)
 
 
+def tail_of(buf, d, c, n=1):
+    return buf.at[d, 64 * c : 64 * (c + n), :]
+
+
 def stage_out_grad(R, C):
     da = R.DA[...].reshape(R.otok.shape[0], R.DA.shape[2])
-    for pr in range(R.otok.shape[1] // 128):
-        cut = slice(pr * 128, pr * 128 + 128)
-        R.gO[cut, :] = mm_at(R.otok[:, cut], da).astype(BF)
-
-
-def stage_attend_back(R, C, n):
+    ho = R.otok.shape[1] // 2
+    k0 = R.G.shape[1] - 8
+    for own, who in ((False, 1 - C.x), (True, C.x)):
+        v = mm_at(R.otok[:, pl.ds(al(who * ho, ho), ho)], da)
+        for d in range(2):
+            for c in range(2):
+                r = d * 64 + c * 32
+                put_wide(R.G.at[d, k0 + c] if own else tail_of(R.A, d, c), v[r : r + 32])
+
+
+def add_tail(R, c0, n):
+    k0 = R.G.shape[1] - 8
+
+    def one(c):
+        for d in range(2):
+            v = R.G[d, k0 + c0 + c].astype(F32) + R.wi[d, pl.ds(al((c0 + c) * 64, 64), 64), :].astype(F32)
+            R.G[d, k0 + c0 + c] = v.astype(BF)
+
+    loop(n, one)
+
+
+def stage_attend_back(R, C, n, ring):
     lo2 = lanes(128) < 64
     ln2 = lanes(128)
 
@@ -525,8 +558,11 @@
     R.dq[...] = jnp.zeros_like(R.dq)
     k = C.sems(n)
     k2 = C.sems(n)
+    base = ring.take(2 * nt)
+    kvs, kvr, dqr = R.asend.at[:, 0:256], R.arecv.at[:, 0:256], R.arecv.at[:, 256:384]
 
     def keys(jj):
+        ring.tick(base + 2 * jj)
         j = nt - 1 - jj
         kat = pl.ds(al(j * T, T), T)
         kk, vv = R.K[kat, :], R.V[kat, :]
@@ -553,11 +589,13 @@
         kv = jnp.where(lo, dk, roll64(dv)).astype(BF)
         for u in range(2):
             b = j * 2 + u
-            R.kvs[b] = kv[u * 256 : u * 256 + 256]
+            R.asend[b, 0:256, :] = kv[u * 256 : u * 256 + 256]
 
             @pl.when(b != C.dp)
             def _():
-                C.rc(R.kvs.at[b], R.kvr.at[C.dp], k + b, (b, C.t), k + C.dp).start()
+                C.rc(kvs.at[b], kvr.at[C.dp], k + b, (b, C.t), k + C.dp).start()
+
+        ring.tick(base + 2 * jj + 1)
 
     loop(nt, keys)
 
@@ -569,14 +607,15 @@
 
         @pl.when(b != C.dp)
         def _():
-            C.rc(R.osend.at[b], R.dqrecv.at[C.dp], k2 + b, (b, C.t), k2 + C.dp).start()
+            C.rc(R.osend.at[b], dqr.at[C.dp], k2 + b, (b, C.t), k2 + C.dp).start()
 
     loop(n, queries)
-    for src, dst, i in ((R.osend, R.dqrecv, 0), (R.kvs, R.kvr, 1)):
+    ring.run(2)
+    for src, dst, i in ((R.osend, dqr, 0), (kvs, kvr, 1)):
         mine = pltpu.make_async_copy(src.at[C.dp], dst.at[C.dp], C.lsem.at[i])
         mine.start()
         mine.wait()
-    for src, dst, kk in ((R.kvs, R.kvr, k), (R.osend, R.dqrecv, k2)):
+    for src, dst, kk in ((kvs, kvr, k), (R.osend, dqr, k2)):
         for b in range(n):
 
             @pl.when(b != C.dp)
@@ -591,10 +630,10 @@
         for pr in range(hp // 2):
             p = s * hp + 2 * pr
             cut = slice(pr * 128, pr * 128 + 128)
-            e, d = R.kvr[p].astype(F32), R.kvr[p + 1].astype(F32)
+            e, d = kvr[p].astype(F32), kvr[p + 1].astype(F32)
             R.dproj[1, s * 256 : s * 256 + 256, cut] = jnp.where(lo, e, roll64(d)).astype(BF)
             R.dproj[2, s * 256 : s * 256 + 256, cut] = jnp.where(lo, roll64(e), d).astype(BF)
-    unfold_heads(R.dqrecv, R.dproj.at[0], n, seqs)
+    unfold_heads(dqr, R.dproj.at[0], n, seqs)
 
 
 def stage_qkv_back(R, C):
@@ -616,139 +655,215 @@
 
 
 def stage_qkv_grad(R, C):
-    def cols(i):
-        at = pl.ds(al(i * 128, 128), 128)
-        h = R.h1[:, at]
-        for m in range(3):
-            R.gQ[m, at, :] = mm_at(h, R.dproj[m]).astype(BF)
-
-    loop(R.h1.shape[1] // 128, cols)
-
-
-class Line:
-    def __init__(self, C, nz, n, src, land, out, locals_at):
-        self.C, self.nz, self.n = C, nz, n
-        self.src, self.land, self.out = src, land, out
-        self.red, self.bc, self.xs = C.sems(2 * n), C.sems(2 * n), C.sems(2 * n)
-        self.loc = locals_at
-
-    def place(self, d):
-        C = self.C
-        step = 1 if d == 0 else -1
-        pos = C.z if d == 0 else self.nz - 1 - C.z
-        up = (C.dp + 2 * step, C.t)
-        down = (C.dp - 2 * step, C.t)
-        return pos, up, down
-
-    def copies(self, d, k):
-        C = self.C
-        pos, up, down = self.place(d)
-        i = d * self.n + k
-        mine = self.out(C.x, d, k)
-        return pos, dict(
-            red=lambda: C.rc(self.src(d, k), self.land(d, k), self.red + i, up),
-            bc_src=lambda: C.rc(self.src(d, k), mine, self.bc + i, down),
-            bc_out=lambda: C.rc(mine, mine, self.bc + i, down),
-            xs_src=lambda: C.rc(self.src(d, k), mine, self.xs + i, C.xp),
-            xs_out=lambda: C.rc(mine, mine, self.xs + i, C.xp),
-            xs_in=lambda: C.rc(self.out(1 - C.x, d, k), self.out(1 - C.x, d, k), self.xs + i, C.xp),
-            keep=lambda: pltpu.make_async_copy(self.src(d, k), mine, C.lsem.at[self.loc + i]),
-        )
-
-    def reduce(self, d, k):
-        pos, c = self.copies(d, k)
-
-        @pl.when(pos > 0)
+    hq = R.h1.shape[1] // 2
+    k = C.sems(2)
+    cps = []
+    k0 = R.G.shape[1] - 6
+    for own, who in ((False, 1 - C.x), (True, C.x)):
+        for d in range(2):
+            for c in range(2):
+                at = pl.ds(al(who * hq + (2 * d + c) * 128, 128), 128)
+                h = R.h1[:, at]
+                for m in range(3):
+                    v = mm_at(h, R.dproj[m]).astype(BF)
+                    w = v.shape[1]
+                    i = 2 * m + c
+                    dst = R.G.at[d, k0 + i] if own else tail_of(R.A, d, 2 + i)
+                    dst[:, 0:w] = v[0:64]
+                    dst[:, w : 2 * w] = v[64:128]
+            if not own:
+                cps.append(C.send(tail_of(R.A, d, 2, 6), tail_of(R.wi, d, 2, 6), k + d, C.xp))
+    return cps
+
+
+class Kinds:
+    def __init__(self, nb, ni):
+        self.i0 = nb
+        self.o0 = nb + ni
+        self.q0 = self.o0 + 2
+        self.n = self.q0 + 6
+
+    def emit(self, R, buf, h, d, k, sem):
+        half = buf.shape[1]
+
+        def put(src, dst):
+            pltpu.make_async_copy(src, dst, sem).start()
+
+        def wide(out, row):
+            at = pl.ds(al(row, 32), 32)
+            put(buf.at[0:32, :], out.at[at, 0:half])
+            put(buf.at[32:64, :], out.at[at, half : 2 * half])
+
+        @pl.when(k < self.i0)
         def _():
-            c["red"]().wait_recv()
-            s, l = self.src(d, k), self.land(d, k)
-            rows = s.shape[0]
-
-            def add(i):
-                at = pl.ds(al(i * 16, 16), 16)
-                s[at, :] = (s[at, :].astype(F32) + l[at, :].astype(F32)).astype(BF)
-
-            loop(rows // 16, add)
-
-        @pl.when(pos < self.nz - 1)
+            wide(R.oB.at[d], h * (self.i0 * 32) + k * 32)
+
+        @pl.when(jnp.logical_and(k >= self.i0, k < self.o0))
         def _():
-            c["red"]().start()
-
-        @pl.when(pos == self.nz - 1)
+            at = pl.ds(al((k - self.i0) * 64, 64), 64)
+            put(buf, R.oI.at[d, at, pl.ds(al(h * half, half), half)])
+
+        @pl.when(jnp.logical_and(k >= self.o0, k < self.q0))
         def _():
-            c["bc_src"]().start()
-            c["xs_src"]().start()
-            c["keep"]().start()
-
-    def spread(self, d, k):
-        pos, c = self.copies(d, k)
-
-        @pl.when(pos < self.nz - 1)
+            wide(R.oO, h * 128 + d * 64 + (k - self.o0) * 32)
+
+        @pl.when(k >= self.q0)
         def _():
-            c["bc_out"]().wait_recv()
-
-            @pl.when(pos > 0)
+            c = k - self.q0
+            m = c // 2
+            row = h * 512 + d * 256 + (c - 2 * m) * 128
+            w = half // 2
+            put(buf.at[:, 0:w], R.oQ.at[m, pl.ds(al(row, 64), 64), :])
+            put(buf.at[:, w : 2 * w], R.oQ.at[m, pl.ds(al(row + 64, 64), 64), :])
+
+
+class Ring:
+    def __init__(self, R, C, K, w):
+        self.R, self.C, self.K, self.w = R, C, K, w
+        n = K.n
+        self.a, self.b, self.x = C.sems(2 * n), C.sems(2 * n), C.sems(2 * n)
+        self.cur = 0
+        self.total = n + 5 * w + 1
+
+    def take(self, n):
+        base = self.cur
+        self.cur += n
+        return base
+
+    def run(self, n):
+        base = self.take(n)
+        loop(n, lambda i: self.tick(base + i))
+
+    def slot(self, buf, d, par, kind):
+        sem = self.C.lsem.at[4 + kind * 4 + d * 2 + par]
+        return pltpu.make_async_copy(buf.at[d, par], buf.at[d, par], sem)
+
+    def xb(self, d, par):
+        return self.R.A.at[d, pl.ds(al(512 + 64 * par, 64), 64), :]
+
+    def tick(self, s):
+        for d in range(2):
+            self.half(s, d)
+
+    def half(self, s, d):
+        R, C, K, w = self.R, self.C, self.K, self.w
+        n = K.n
+        pos = C.z if d == 0 else 3 - C.z
+
+        def dev(p):
+            return ((p if d == 0 else 3 - p) * 2 + C.x, C.t)
+
+        def act(k, cond):
+            ok = jnp.logical_and(k >= 0, k < n)
+            return ok if cond is None else jnp.logical_and(ok, cond)
+
+        @pl.when(act(s, jnp.logical_or(pos == 0, pos == 3)))
+        def _():
+            i = d * n + s
+            C.rc(R.G.at[d, s], R.L1.at[d, s], self.a + i, dev(1 + pos // 3)).start()
+
+        k2 = s - w
+
+        @pl.when(act(k2, pos == 2))
+        def _():
+            i = d * n + k2
+            C.rc(R.G.at[d, k2], R.L1.at[d, k2], self.a + i, dev(1)).wait_recv()
+            R.G[d, k2] = (R.G[d, k2].astype(F32) + R.L1[d, k2].astype(F32)).astype(BF)
+            C.rc(R.G.at[d, k2], R.FN.at[d, k2], self.a + i, dev(1), self.b + i).start()
+
+        k1 = s - 2 * w
+
+        @pl.when(act(k1, pos == 1))
+        def _():
+            i = d * n + k1
+            fn = R.FN.at[d, k1]
+            C.rc(R.G.at[d, k1], R.L1.at[d, k1], self.a + i, dev(0)).wait_recv()
+            C.rc(fn, fn, self.b + i, dev(2)).wait_recv()
+            v = R.G[d, k1].astype(F32) + R.L1[d, k1].astype(F32) + R.FN[d, k1].astype(F32)
+            R.FN[d, k1] = v.astype(BF)
+            C.rc(fn, fn, self.b + i, dev(2)).start()
+            C.rc(fn, fn, self.a + i, dev(0), self.b + i).start()
+
+        lag = w * (2 + jnp.where(pos == 1, 0, 1) + jnp.where(pos == 3, 1, 0))
+        kf = s - lag
+
+        @pl.when(act(kf, None))
+        def _():
+            i = d * n + kf
+            fn = R.FN.at[d, kf]
+
+            @pl.when(pos != 1)
             def _():
-                c["bc_out"]().start()
-
-            c["xs_out"]().start()
+                C.rc(fn, fn, self.b + i, dev(1)).wait_recv()
+
+            @pl.when(pos == 2)
+            def _():
+                C.rc(fn, fn, self.b + i, dev(3)).start()
+
+            C.rc(fn, R.XH.at[d, kf], self.x + i, C.xp).start()
+            self.store(R.FN.at[d, kf], R.SF, 0, C.x, d, kf)
+
+        kx = kf - w
+
+        @pl.when(act(kx, None))
+        def _():
+            xh = R.XH.at[d, kx]
+            C.rc(xh, xh, self.x + d * n + kx, C.xp).wait_recv()
+            par = lax.rem(kx, 2)
+            pltpu.make_async_copy(xh, self.xb(d, par), C.lsem.at[12 + d * 2 + par]).start()
+
+        ky = kx - 1
+
+        @pl.when(act(ky, None))
+        def _():
+            par = lax.rem(ky, 2)
+            xb = self.xb(d, par)
+            pltpu.make_async_copy(R.XH.at[d, ky], xb, C.lsem.at[12 + d * 2 + par]).wait()
+            self.store(xb, R.SX, 1, 1 - C.x, d, ky)
+
+    def store(self, src, buf, kind, h, d, k):
+        par = lax.rem(k, 2)
+
+        @pl.when(k >= 2)
+        def _():
+            self.slot(buf, d, par, kind).wait()
+
+        buf[d, par] = src[...].astype(F32)
+        self.K.emit(self.R, buf.at[d, par], h, d, k, self.C.lsem.at[4 + kind * 4 + d * 2 + par])
 
     def finish(self):
+        R, C, n = self.R, self.C, self.K.n
+
         def one(k):
             for d in range(2):
-                pos, c = self.copies(d, k)
-                c["xs_in"]().wait_recv()
-                c["xs_out"]().wait_send()
-
-                @pl.when(pos < self.nz - 1)
+                i = d * n + k
+                pos = C.z if d == 0 else 3 - C.z
+                fn = R.FN.at[d, k]
+                C.rc(fn, fn, self.a + i, C.xp).wait_send()
+                C.rc(fn, fn, self.x + i, C.xp).wait_send()
+
+                @pl.when(jnp.logical_or(pos == 1, pos == 2))
                 def _():
-                    c["red"]().wait_send()
-
-                @pl.when(pos > 0)
-                def _():
-                    c["bc_out"]().wait_send()
-
-                @pl.when(pos == self.nz - 1)
-                def _():
-                    c["keep"]().wait()
-
-        loop(self.n, one)
-
-
-def exchange_x(C, full, land, half):
-    k = C.sems(1)
-    lead = (slice(None),) * (len(full.shape) - 2)
-    theirs = pl.ds(al((1 - C.x) * half, half), half)
-    cp = C.send(full.at[lead + (theirs,)], land, k, C.xp)
-
-    def wait():
-        cp.wait_recv()
-        groups = full.shape[0] if lead else 1
-        for m in range(groups):
-
-            def add(i):
-                at = pl.ds(al(i * 16, 16), 16)
-                own = pl.ds(al(C.x * half + i * 16, 16), 16)
-                if lead:
-                    v = full[m, own, :].astype(F32) + land[m, at, :].astype(F32)
-                    full[m, own, :] = v.astype(BF)
-                else:
-                    v = full[own, :].astype(F32) + land[at, :].astype(F32)
-                    full[own, :] = v.astype(BF)
-
-            loop(half // 16, add)
-
-    return wait
-
-
-def stage_small(R, C, n):
+                    C.rc(fn, fn, self.b + i, C.xp).wait_send()
+
+        loop(n, one)
+        for d in range(2):
+            for par in range(2):
+                self.slot(R.SF, d, par, 0).wait()
+                self.slot(R.SX, d, par, 1).wait()
+
+
+def small_tensor(R, C):
     R.st[C.t, 0:8, :] = R.sm[...]
     R.st[C.t, 8:16, :] = R.sm2[...]
     k = C.sems(3)
-    cps = [
+    return [
         C.send(R.st.at[C.t], R.st.at[C.t], k + i, dev)
         for i, dev in enumerate((C.mate, C.yp, (C.dp, 3 - C.t)))
     ]
+
+
+def small_dp(R, C, n, cps):
     for cp in cps:
         cp.wait_recv()
     tot = R.st[0] + R.st[1] + R.st[2] + R.st[3]
@@ -766,9 +881,10 @@
     for e in range(2):
         sd[11:12, e * half : (e + 1) * half] = rowsum(R.DH[e].astype(F32))
     k = C.sems(n)
-    cps = [
-        C.send(sd, R.sd.at[C.dp], k + o, (lax.rem(C.dp + o, n), C.t)) for o in range(1, n)
-    ]
+    return [C.send(sd, R.sd.at[C.dp], k + o, (lax.rem(C.dp + o, n), C.t)) for o in range(1, n)]
+
+
+def small_end(R, C, n, cps):
     for cp in cps:
         cp.wait_recv()
     tot = R.sd[0]
@@ -786,10 +902,10 @@
     pass
 
 
-ROWS_B, ROWS_I = 64, 128
-
-
-def body(names, n, nz, *refs):
+LAG = 3
+
+
+def body(names, n, *refs):
     R = Refs()
     for name, ref in zip(names, refs):
         setattr(R, name, ref)
@@ -814,80 +930,44 @@
     for cp in wcp:
         cp.wait()
     stage_moe(R, C)
+    K = Kinds(half // 32, R.H2.shape[2] // 64)
+    ring = Ring(R, C, K, LAG)
     wait_u = reduce8(R, C, R.YP, R.ly, R.sy, R.u)
     wait_x = reduce8(R, C, R.DXP, R.lx, R.sx, R.dx)
-    stage_moe_grads(R, C)
-
-    lb = Line(
-        C, nz, half // ROWS_B,
-        lambda d, k: R.gB.at[d, pl.ds(al(k * ROWS_B, ROWS_B), ROWS_B), :],
-        lambda d, k: R.lB.at[d, pl.ds(al(k * ROWS_B, ROWS_B), ROWS_B), :],
-        lambda h, d, k: R.oB.at[d, pl.ds(al(h * half + k * ROWS_B, ROWS_B), ROWS_B), :],
-        4,
-    )
-    D = R.gI.shape[1]
-    li = Line(
-        C, nz, D // ROWS_I,
-        lambda d, k: R.gI.at[d, pl.ds(al(k * ROWS_I, ROWS_I), ROWS_I), :],
-        lambda d, k: R.lI.at[d, pl.ds(al(k * ROWS_I, ROWS_I), ROWS_I), :],
-        lambda h, d, k: R.oI.at[
-            d, pl.ds(al(k * ROWS_I, ROWS_I), ROWS_I), pl.ds(al(h * half, half), half)
-        ],
-        4 + 2 * lb.n,
-    )
-
+    stage_moe_grads(R, C, K, ring)
     wait_u()
+    ring.run(2)
     wait_x()
     stage_owner(R, C)
     wait_da = gather4(R, C, R.DA)
     wait_res = gather4(R, C, R.RES)
+    ring.run(3)
     wait_da()
     stage_out_back(R, C, n)
     wait_do = all_to_all(R, C, R.osend, R.dorecv, n)
     stage_out_grad(R, C)
+    xo = C.send(R.A.at[:, 0:128, :], R.wi.at[:, 0:128, :], C.sems(1), C.xp)
+    ring.run(3)
     wait_do()
     C.drain()
-    stage_attend_back(R, C, n)
+    stage_attend_back(R, C, n, ring)
     stage_qkv_back(R, C)
     wait_gin = gather4(R, C, R.GIN)
-    stage_qkv_grad(R, C)
-    F = R.gO.shape[0]
-    hq, ho = D // 2, F // 2
-    wq = exchange_x(C, R.gQ, R.xQ, hq)
-    wo = exchange_x(C, R.gO, R.xO, ho)
-    wq()
-    wo()
+    small = small_tensor(R, C)
+    ring.run(2)
+    xq = stage_qkv_grad(R, C)
+    small = small_dp(R, C, n, small)
+    xo.wait_recv()
+    add_tail(R, 0, 2)
+    ring.run(K.o0 - ring.cur)
+    for cp in xq:
+        cp.wait_recv()
+    add_tail(R, 2, 6)
     wait_gin()
     wait_res()
-    qd, od = hq // 2, ho // 2
-    lq = Line(
-        C, nz, 3,
-        lambda d, k: R.gQ.at[k, pl.ds(al(C.x * hq + d * qd, qd), qd), :],
-        lambda d, k: R.lQ.at[d, k],
-        lambda h, d, k: R.oQ.at[k, pl.ds(al(h * hq + d * qd, qd), qd), :],
-        4 + 2 * lb.n + 2 * li.n,
-    )
-    lo = Line(
-        C, nz, 1,
-        lambda d, k: R.gO.at[pl.ds(al(C.x * ho + d * od, od), od), :],
-        lambda d, k: R.lO.at[d],
-        lambda h, d, k: R.oO.at[pl.ds(al(h * ho + d * od, od), od), :],
-        4 + 2 * lb.n + 2 * li.n + 6,
-    )
-    work = [(L, k) for L in (lb, li, lq, lo) for k in range(L.n)]
-    lag = 4
-    for s in range(len(work) + lag):
-        if s < len(work):
-            L, k = work[s]
-            L.reduce(0, k)
-            L.reduce(1, k)
-        if s >= lag:
-            L, k = work[s - lag]
-            L.spread(0, k)
-            L.spread(1, k)
-    stage_small(R, C, n)
-    for L in (lb, li, lq, lo):
-        L.finish()
+    ring.run(ring.total - ring.cur)
+    small_end(R, C, n, small)
+    ring.finish()
     C.drain()
 
 
@@ -899,7 +979,6 @@
     F = w_qkv.shape[2]
     H = w_in.shape[2]
     half = H // 2
-    nz = n // 2
     total = n * span
     par = jnp.concatenate(
         [jnp.stack([g1, b1, out_b, g2, b2]), router.T, back_b, jnp.zeros((7, D), BF)], axis=0
@@ -920,17 +999,18 @@
         ("w_back", w_back, hbm),
     ]
     sds = jax.ShapeDtypeStruct
+    nch = half // 32 + D // 64 + 8
     outs = [
         ("RES", sds((nt, CH, D), BF), vm),
         ("GIN", sds((nt, CH, D), BF), vm),
-        ("oB", sds((2, H, D), BF), hbm),
-        ("oI", sds((2, D, H), BF), hbm),
-        ("oQ", sds((3, D, F), BF), hbm),
-        ("oO", sds((F, D), BF), hbm),
+        ("oB", sds((2, H, D), F32), hbm),
+        ("oI", sds((2, D, H), F32), hbm),
+        ("oQ", sds((3, D, F), F32), hbm),
+        ("oO", sds((F, D), F32), hbm),
+        ("XH", sds((2, nch, 64, 512), BF), hbm),
         ("osm", sds((16, D), F32), vm),
     ]
     V = pltpu.VMEM
-    nch = half // ROWS_B + D // ROWS_I + 4
     scr = [
         ("h1", V((rows, D), BF)),
         ("asend", V((n, 384, 128), BF)),
@@ -944,9 +1024,6 @@
         ("osend", V((n, 128, 128), BF)),
         ("orecv", V((n, 128, 128), BF)),
         ("dorecv", V((n, 128, 128), BF)),
-        ("dqrecv", V((n, 128, 128), BF)),
-        ("kvs", V((n, 256, 128), BF)),
-        ("kvr", V((n, 256, 128), BF)),
         ("otok", V((rows, F), BF)),
         ("dproj", V((3, rows, F), BF)),
         ("p4", V((3, CH, D), BF)),
@@ -969,27 +1046,22 @@
         ("sy", V((3, CH, D), BF)),
         ("sx", V((3, CH, D), BF)),
         ("DA", V((nt, CH, D), BF)),
-        ("gB", V((2, half, D), BF)),
-        ("gI", V((2, D, half), BF)),
-        ("gQ", V((3, D, F), BF)),
-        ("gO", V((F, D), BF)),
-        ("lB", V((2, half, D), BF)),
-        ("lI", V((2, D, half), BF)),
-        ("xQ", V((3, D // 2, F), BF)),
-        ("xO", V((F // 2, D), BF)),
-        ("lQ", V((2, 3, D // 4, F), BF)),
-        ("lO", V((2, F // 4, D), BF)),
+        ("G", V((2, nch, 64, 512), BF)),
+        ("L1", V((2, nch, 64, 512), BF)),
+        ("FN", V((2, nch, 64, 512), BF)),
+        ("SF", V((2, 2, 64, 512), F32)),
+        ("SX", V((2, 2, 64, 512), F32)),
         ("sm", V((8, D), F32)),
         ("sm2", V((8, D), F32)),
         ("st", V((4, 16, D), F32)),
         ("sd", V((n, 16, D), F32)),
-        ("ssem", pltpu.SemaphoreType.DMA((120 + 6 * nch,))),
-        ("rsem", pltpu.SemaphoreType.DMA((120 + 6 * nch,))),
-        ("lsem", pltpu.SemaphoreType.DMA((8 + 2 * nch,))),
+        ("ssem", pltpu.SemaphoreType.DMA((128 + 6 * nch,))),
+        ("rsem", pltpu.SemaphoreType.DMA((128 + 6 * nch,))),
+        ("lsem", pltpu.SemaphoreType.DMA((16,))),
     ]
     names = [i[0] for i in ins] + [o[0] for o in outs] + [s[0] for s in scr]
-    res, gin, oB, oI, oQ, oO, osm = pl.pallas_call(
-        functools.partial(body, names, n, nz),
+    res, gin, oB, oI, oQ, oO, _, osm = pl.pallas_call(
+        functools.partial(body, names, n),
         out_shape=[o[1] for o in outs],
         in_specs=[i[2] for i in ins],
         out_specs=[o[2] for o in outs],
@@ -1005,16 +1077,16 @@
         gin.reshape(S, span, D).astype(F32),
         osm[8],
         osm[9],
-        oQ.astype(F32).transpose(1, 0, 2),
+        oQ.transpose(1, 0, 2),
         osm[10, : 2 * F].reshape(2, F),
-        oO.astype(F32),
+        oO,
         osm[2],
         osm[0],
         osm[1],
         osm[3:5].T,
-        oI.astype(F32),
+        oI,
         inb,
-        oB.astype(F32),
+        oB,
         osm[5:7],
     )
 
@@ -1446,7 +1518,10 @@
         heads = w_qkv.shape[2] // HEAD_DIM
         fits = (
             nt == 4
-            and n % 2 == 0
+            and n == 8
+            and tokens.shape[2] == 1024
+            and w_qkv.shape[2] == 256
+            and args[10].shape == (2, 1024, 1024)
             and n == tokens.shape[0] * heads
             and tokens.shape[0] * tokens.shape[1] == nt * CH
             and tokens.shape[1] == 256

time: 857 us -> 333 us (0.39)
  Pallas kernels: 824 us -> 302 us
  other arithmetic: 19.5 us -> 5.35 us
  local copies, waits for them, and re-layouts: 9.32 us -> 23.4 us
    pallas_call x1, Pallas kernels: 824 us -> 302 us  [fast_local(): pl.pallas_call(functools.partial(body, names, n), out_shape=[o[1] for o i...]
    unnamed x6 -> x14, local copies, waits for them, and re-layouts: 0.01 us -> 13.9 us
    convert_element_type x3 -> x0, other arithmetic: 12.3 us -> none  [the longest x1 6.79 us: fast_local(): oI.astype(F32)]
where the time goes in v2:
time: 333 us; the launch traced here: 332 us
  Pallas kernels  302 us (91%)
  local copies, waits for them, and re-layouts  23.4 us (7%)
  other arithmetic  5.35 us (2%)
    pallas_call x1, Pallas kernels, fast_local(): pl.pallas_call(functools.partial(body, names, n), out_shape=[o[1] for o i...  302 us
    unnamed x14, local copies, waits for them, and re-layouts  13.9 us

profile of v2, /device:TPU:0, one launch (start us, length us, event | category | flops | bytes accessed | tf_op | source)
XLA Modules:
  0.0 331.8 jit_solution(18283305282421238346)
XLA Ops:
  0.6 0.7 stack.18
  1.3 0.7 stack.19
  2.0 0.7 stack.20
  2.7 0.7 stack.21
  3.4 0.7 stack.22
  4.1 1.6 concatenate.3
  5.6 0.6 convert_element_type.15.refs_1_
  6.3 302.4 %layer.1 = (bf16[4,128,1024]{2,1,0:T(8,128)(2,1)}, bf16[4,128,1024]{2,1,0:T(8,128)(2,1)}, f32[2,1024,1024]{2,1,0:T(8,128)}, f32[2,1024,1024]{2,1,0:T(8,128)}, f3...) custom-call(bf16[512,1024]{1,0:T(8,128)(2,1)} %bitcast.27, ...), custom_call_target="tpu_custom_call" | custom-call | tf_op jit(solution)/shard_map/layer/pallas_call | solution.py:1063
  308.7 0.0 copy-start.1
  308.7 0.9 slice_reduce_fusion.2
  309.6 0.6 reshape_squeeze.3
  310.1 1.4 fusion
  311.6 1.6 slice_reduce_fusion.1
  313.2 0.6 pad_maximum_fusion
  313.8 0.0 copy-start.2
  313.8 4.1 %bitcast_convert_fusion = (f32[2,256,1024]{2,1,0:T(8,128)}, f32[2,256,1024]{2,1,0:T(8,128)}) fusion(bf16[2,256,1024]{2,1,0:T(8,128)(2,1)} %bitcast.26, bf16[2,256,1024]{2,1,0:T(8,128)(2,1)} %bitcast.25), kind=kLoop, calls=%fused_computation | loop fusion | flops 1048576 | bytes 6291456 | tf_op jit(solution)/shard_map/convert_element_type | solution.py:1077
  317.9 0.0 copy-start
  317.9 0.0 copy-done.1
  317.9 1.7 copy.37
  319.5 0.0 copy-done.2
  319.5 0.0 slice-start
  319.5 1.0 copy.38
  320.5 2.3 copy-done
  322.8 0.0 slice-start.1
  322.8 4.3 %copy.39 = f32[2,1024,1024]{2,1,0:T(8,128)} copy(f32[2,1024,1024]{2,1,0:T(8,128)S(1)} %copy-done) | data formatting | bytes 16777216
  327.0 0.0 slice-done
  327.0 1.4 slice-done.1
  328.4 3.4 %copy.40 = f32[2,1024,1024]{2,1,0:T(8,128)} copy(f32[2,1024,1024]{2,1,0:T(8,128)S(1)} %bitcast.22) | data formatting | bytes 16777216
  (4 shorter events, 0.0 us)
Async XLA Ops:
  308.7 9.2 %copy-start.1 = (f32[3,1024,256]{2,1,0:T(8,128)S(1)}, f32[3,1024,256]{2,1,0:T(8,128)}, u32[]{:S(2)}) copy-start(f32[3,1024,256]{2,1,0:T(8,128)} %get-tuple-element.25) | copy-start | bytes 9437188
  313.8 5.8 %copy-start.2 = (f32[256,1024]{1,0:T(8,128)S(1)}, f32[256,1024]{1,0:T(8,128)}, u32[]{:S(2)}) copy-start(f32[256,1024]{1,0:T(8,128)} %get-tuple-element.61) | copy-start | bytes 3145732
  317.9 4.9 %copy-start = (f32[2,1024,1024]{2,1,0:T(8,128)S(1)}, f32[2,1024,1024]{2,1,0:T(8,128)}, u32[]{:S(2)}) copy-start(f32[2,1024,1024]{2,1,0:T(8,128)} %get-tuple-element.66) | copy-start | bytes 25165828
  319.5 7.5 %slice-start = ((s8[8388608]{0:T(1024)(128)(4,1)}), s8[4194304]{0:T(1024)(128)(4,1)S(1)}, s32[]{:S(2)}) async-start(s8[8388608]{0:T(1024)(128)(4,1)} %bitcast.21), calls=%async_computation | async-start | bytes 8388608
  322.8 5.6 %slice-start.1 = ((s8[8388608]{0:T(1024)(128)(4,1)}), s8[4194304]{0:T(1024)(128)(4,1)S(1)}, s32[]{:S(2)}) async-start(s8[8388608]{0:T(1024)(128)(4,1)} %bitcast.21), calls=%async_computation.1 | async-start | bytes 8388608

commit v3 on v2

--- a/solution.py
+++ b/solution.py
@@ -114,19 +114,19 @@
     return cent * r, r
 
 
-def stage_qkv(R, C):
+def stage_qkv(R, C, n):
     rows = R.tok.shape[0]
     gain, bias = R.par[0:1, :], R.par[1:2, :]
-
-    def ln(i):
-        at = pl.ds(al(i * 32, 32), 32)
-        n, _ = norm_parts(R.tok[at, :].astype(F32))
-        R.h1[at, :] = (n * gain + bias).astype(BF)
-
-    loop(rows // 32, ln)
     hp = R.wqkv.shape[2] // HEAD_DIM
+    k = C.sems(n)
 
     def seq(s):
+        def ln(i):
+            at = pl.ds(al(s * 256 + i * 32, 32), 32)
+            n1, _ = norm_parts(R.tok[at, :].astype(F32))
+            R.h1[at, :] = (n1 * gain + bias).astype(BF)
+
+        loop(8, ln)
         at = pl.ds(al(s * 256, 256), 256)
         h = R.h1[at, :]
         lo = lanes(256) < 64
@@ -142,8 +142,30 @@
             a, b = tv[0:128], tv[128:256]
             R.asend[p, 256:384, :] = jnp.where(lo2, a, roll64(b)).astype(BF)
             R.asend[p + 1, 256:384, :] = jnp.where(lo2, roll64(a), b).astype(BF)
+            for j in range(2):
+                send_slice(C, R.asend, R.arecv, k, p + j)
 
     loop(rows // 256, seq)
+    return lambda: wait_slices(C, R.asend, R.arecv, k, n, 0)
+
+
+def send_slice(C, src, dst, k, p):
+    @pl.when(p != C.dp)
+    def _():
+        C.rc(src.at[p], dst.at[C.dp], k + p, (p, C.t), k + C.dp).start()
+
+
+def wait_slices(C, src, dst, k, n, sem):
+    mine = pltpu.make_async_copy(src.at[C.dp], dst.at[C.dp], C.lsem.at[sem])
+    mine.start()
+    mine.wait()
+    for b in range(n):
+
+        @pl.when(b != C.dp)
+        def _():
+            cp = C.rc(src.at[b], dst.at[b], k + b, (b, C.t), k + b)
+            cp.wait_send()
+            cp.wait_recv()
 
 
 def all_to_all(R, C, src, dst, n):
@@ -246,6 +268,19 @@
             cut = slice(pr * 128, pr * 128 + 128)
             dst[s * 256 : s * 256 + 128, cut] = jnp.where(lo2, e, roll64(d)).astype(BF)
             dst[s * 256 + 128 : s * 256 + 256, cut] = jnp.where(lo2, roll64(e), d).astype(BF)
+
+
+def swap_cot(R, C):
+    k = C.sems(2)
+    rows = R.cot.shape[0] // 2
+    mine = pl.ds(al(C.c * rows, rows), rows)
+    cp = C.send(R.cot.at[mine, :], R.cx.at[mine, :], k, C.xp)
+
+    def wait():
+        cp.wait_recv()
+        C.send(R.cx.at[mine, :], R.cx.at[mine, :], k + 1, C.mate).wait_recv()
+
+    return wait
 
 
 def reduce4(R, C, part, out):
@@ -338,19 +373,30 @@
     p0, p1 = e0 / (e0 + e1), e1 / (e0 + e1)
     gate = here[:, 0:1] * p0 + here[:, 1:2] * p1
     ln = lanes(CH)
-    R.META[slot] = jnp.where(ln == 0, keep0, jnp.where(ln == 1, keep1, 0.0)).astype(BF)
+    hi = gate.astype(BF).astype(F32)
+    mid = (gate - hi).astype(BF).astype(F32)
+    meta = jnp.zeros((CH, 128), F32)
+    for i, v in enumerate((keep0, keep1, hi, mid, gate - hi - mid)):
+        meta = jnp.where(ln == i, v, meta)
+    R.META[slot] = meta.astype(BF)
     wait_h = gather8(R, C, R.H2)
     wait_m = gather8(R, C, R.META)
-    gr = (gate * R.cot[own, :].astype(F32)).astype(BF)
-    R.GG[slot] = (gr.astype(F32) * (keep0 + keep1)).astype(BF)
-    wait_g = gather8(R, C, R.GG)
     cols = jnp.zeros((CH, 128), F32)
     for i, v in enumerate((p0, p1, here[:, 0:1], here[:, 1:2], gate, keep0, keep1)):
         cols = jnp.where(ln == i, v, cols)
     R.cols[...] = cols
     wait_h()
     wait_m()
-    wait_g()
+
+    def gated(i):
+        for xx, cot in ((C.x, R.cot), (1 - C.x, R.cx)):
+            m = R.META[xx * 4 + i].astype(F32)
+            gate = m[:, 2:3] + m[:, 3:4] + m[:, 4:5]
+            g = cot[pl.ds(al(i * CH, CH), CH), :].astype(F32)
+            gr = (gate * g).astype(BF).astype(F32)
+            R.GG[xx * 4 + i] = (gr * (m[:, 0:1] + m[:, 1:2])).astype(BF)
+
+    loop(4, gated)
 
 
 def gelu_both(h):
@@ -408,7 +454,7 @@
 
     loop(R.A.shape[2] // 128, back)
     ring.run(3)
-    base = ring.take(R.H2.shape[2] // 128)
+    base = ring.take(R.H2.shape[2] // 256)
 
     def into(i):
         at = pl.ds(al(i * 128, 128), 128)
@@ -417,7 +463,10 @@
             v = mm_at(h2t, R.DH[e]).astype(BF)
             R.G[e, K.i0 + 2 * i] = v[0:64]
             R.G[e, K.i0 + 2 * i + 1] = v[64:128]
-        ring.tick(base + i)
+
+        @pl.when(lax.rem(i, 2) == 1)
+        def _():
+            ring.tick(base + i // 2)
 
     loop(R.H2.shape[2] // 128, into)
 
@@ -528,7 +577,7 @@
     loop(n, one)
 
 
-def stage_attend_back(R, C, n, ring):
+def stage_attend_back(R, C, n, ring, xo):
     lo2 = lanes(128) < 64
     ln2 = lanes(128)
 
@@ -610,7 +659,9 @@
             C.rc(R.osend.at[b], dqr.at[C.dp], k2 + b, (b, C.t), k2 + C.dp).start()
 
     loop(n, queries)
-    ring.run(2)
+    xo.wait_recv()
+    add_tail(R, 0, 2)
+    ring.run(T_KV)
     for src, dst, i in ((R.osend, dqr, 0), (kvs, kvr, 1)):
         mine = pltpu.make_async_copy(src.at[C.dp], dst.at[C.dp], C.lsem.at[i])
         mine.start()
@@ -654,7 +705,7 @@
     R.sm2[1:2, :] = rowsum(dh1)
 
 
-def stage_qkv_grad(R, C):
+def stage_qkv_grad(R, C, ring):
     hq = R.h1.shape[1] // 2
     k = C.sems(2)
     cps = []
@@ -671,6 +722,7 @@
                     dst = R.G.at[d, k0 + i] if own else tail_of(R.A, d, 2 + i)
                     dst[:, 0:w] = v[0:64]
                     dst[:, w : 2 * w] = v[64:128]
+            ring.run(T_QG)
             if not own:
                 cps.append(C.send(tail_of(R.A, d, 2, 6), tail_of(R.wi, d, 2, 6), k + d, C.xp))
     return cps
@@ -683,47 +735,35 @@
         self.q0 = self.o0 + 2
         self.n = self.q0 + 6
 
-    def emit(self, R, buf, h, d, k, sem):
-        half = buf.shape[1]
-
-        def put(src, dst):
-            pltpu.make_async_copy(src, dst, sem).start()
-
-        def wide(out, row):
-            at = pl.ds(al(row, 32), 32)
-            put(buf.at[0:32, :], out.at[at, 0:half])
-            put(buf.at[32:64, :], out.at[at, half : 2 * half])
-
-        @pl.when(k < self.i0)
-        def _():
-            wide(R.oB.at[d], h * (self.i0 * 32) + k * 32)
-
-        @pl.when(jnp.logical_and(k >= self.i0, k < self.o0))
-        def _():
-            at = pl.ds(al((k - self.i0) * 64, 64), 64)
-            put(buf, R.oI.at[d, at, pl.ds(al(h * half, half), half)])
-
-        @pl.when(jnp.logical_and(k >= self.o0, k < self.q0))
-        def _():
-            wide(R.oO, h * 128 + d * 64 + (k - self.o0) * 32)
-
-        @pl.when(k >= self.q0)
-        def _():
-            c = k - self.q0
-            m = c // 2
-            row = h * 512 + d * 256 + (c - 2 * m) * 128
-            w = half // 2
-            put(buf.at[:, 0:w], R.oQ.at[m, pl.ds(al(row, 64), 64), :])
-            put(buf.at[:, w : 2 * w], R.oQ.at[m, pl.ds(al(row + 64, 64), 64), :])
+
+class Sums:
+    def __init__(self, R, C, n):
+        self.R, self.C, self.n = R, C, n
+        self.a, self.b = C.sems(2 * n), C.sems(2 * n)
+        self.one = C.sems(6)
+
+    def finish(self):
+        R, C = self.R, self.C
+        for d in range(2):
+            pos = C.z if d == 0 else 3 - C.z
+            fn = R.FN.at[d]
+            C.rc(fn, fn, self.one + d, C.xp).wait_send()
+
+            @pl.when(jnp.logical_or(pos == 1, pos == 2))
+            def _():
+                C.rc(fn, fn, self.one + 2 + d, C.xp).wait_send()
+
+            cp = C.rc(fn, R.XH.at[d], self.one + 4 + d, C.xp)
+            cp.wait_send()
+            cp.wait_recv()
+            pltpu.make_async_copy(fn, R.FH.at[d], C.lsem.at[4 + d]).wait()
 
 
 class Ring:
-    def __init__(self, R, C, K, w):
-        self.R, self.C, self.K, self.w = R, C, K, w
-        n = K.n
-        self.a, self.b, self.x = C.sems(2 * n), C.sems(2 * n), C.sems(2 * n)
+    def __init__(self, sums, k0, k1, w):
+        self.S, self.k0, self.k1, self.w = sums, k0, k1, w
         self.cur = 0
-        self.total = n + 5 * w + 1
+        self.total = k1 - k0 + 4 * w
 
     def take(self, n):
         base = self.cur
@@ -734,42 +774,43 @@
         base = self.take(n)
         loop(n, lambda i: self.tick(base + i))
 
-    def slot(self, buf, d, par, kind):
-        sem = self.C.lsem.at[4 + kind * 4 + d * 2 + par]
-        return pltpu.make_async_copy(buf.at[d, par], buf.at[d, par], sem)
-
-    def xb(self, d, par):
-        return self.R.A.at[d, pl.ds(al(512 + 64 * par, 64), 64), :]
+    def rest(self):
+        self.run(self.total - self.cur)
 
     def tick(self, s):
         for d in range(2):
-            self.half(s, d)
+            self.half(s + self.k0, d)
 
     def half(self, s, d):
-        R, C, K, w = self.R, self.C, self.K, self.w
-        n = K.n
+        S, w = self.S, self.w
+        R, C, n, one = S.R, S.C, S.n, S.one
         pos = C.z if d == 0 else 3 - C.z
 
         def dev(p):
             return ((p if d == 0 else 3 - p) * 2 + C.x, C.t)
 
         def act(k, cond):
-            ok = jnp.logical_and(k >= 0, k < n)
+            ok = jnp.logical_and(k >= self.k0, k < self.k1)
             return ok if cond is None else jnp.logical_and(ok, cond)
+
+        def toward(src, dst, kr, p):
+            return C.rc(src, dst, one + d, dev(p), kr)
+
+        def away(fn, i, p):
+            return C.rc(fn, fn, one + 2 + d, dev(p), S.b + i)
 
         @pl.when(act(s, jnp.logical_or(pos == 0, pos == 3)))
         def _():
-            i = d * n + s
-            C.rc(R.G.at[d, s], R.L1.at[d, s], self.a + i, dev(1 + pos // 3)).start()
+            toward(R.G.at[d, s], R.L1.at[d, s], S.a + d * n + s, 1 + pos // 3).start()
 
         k2 = s - w
 
         @pl.when(act(k2, pos == 2))
         def _():
             i = d * n + k2
-            C.rc(R.G.at[d, k2], R.L1.at[d, k2], self.a + i, dev(1)).wait_recv()
+            toward(R.G.at[d, k2], R.L1.at[d, k2], S.a + i, 1).wait_recv()
             R.G[d, k2] = (R.G[d, k2].astype(F32) + R.L1[d, k2].astype(F32)).astype(BF)
-            C.rc(R.G.at[d, k2], R.FN.at[d, k2], self.a + i, dev(1), self.b + i).start()
+            toward(R.G.at[d, k2], R.FN.at[d, k2], S.b + i, 1).start()
 
         k1 = s - 2 * w
 
@@ -777,12 +818,12 @@
         def _():
             i = d * n + k1
             fn = R.FN.at[d, k1]
-            C.rc(R.G.at[d, k1], R.L1.at[d, k1], self.a + i, dev(0)).wait_recv()
-            C.rc(fn, fn, self.b + i, dev(2)).wait_recv()
+            toward(R.G.at[d, k1], R.L1.at[d, k1], S.a + i, 0).wait_recv()
+            away(fn, i, 2).wait_recv()
             v = R.G[d, k1].astype(F32) + R.L1[d, k1].astype(F32) + R.FN[d, k1].astype(F32)
             R.FN[d, k1] = v.astype(BF)
-            C.rc(fn, fn, self.b + i, dev(2)).start()
-            C.rc(fn, fn, self.a + i, dev(0), self.b + i).start()
+            away(fn, i, 2).start()
+            toward(fn, fn, S.b + i, 0).start()
 
         lag = w * (2 + jnp.where(pos == 1, 0, 1) + jnp.where(pos == 3, 1, 0))
         kf = s - lag
@@ -794,63 +835,14 @@
 
             @pl.when(pos != 1)
             def _():
-                C.rc(fn, fn, self.b + i, dev(1)).wait_recv()
+                away(fn, i, 1).wait_recv()
 
             @pl.when(pos == 2)
             def _():
-                C.rc(fn, fn, self.b + i, dev(3)).start()
-
-            C.rc(fn, R.XH.at[d, kf], self.x + i, C.xp).start()
-            self.store(R.FN.at[d, kf], R.SF, 0, C.x, d, kf)
-
-        kx = kf - w
-
-        @pl.when(act(kx, None))
-        def _():
-            xh = R.XH.at[d, kx]
-            C.rc(xh, xh, self.x + d * n + kx, C.xp).wait_recv()
-            par = lax.rem(kx, 2)
-            pltpu.make_async_copy(xh, self.xb(d, par), C.lsem.at[12 + d * 2 + par]).start()
-
-        ky = kx - 1
-
-        @pl.when(act(ky, None))
-        def _():
-            par = lax.rem(ky, 2)
-            xb = self.xb(d, par)
-            pltpu.make_async_copy(R.XH.at[d, ky], xb, C.lsem.at[12 + d * 2 + par]).wait()
-            self.store(xb, R.SX, 1, 1 - C.x, d, ky)
-
-    def store(self, src, buf, kind, h, d, k):
-        par = lax.rem(k, 2)
-
-        @pl.when(k >= 2)
-        def _():
-            self.slot(buf, d, par, kind).wait()
-
-        buf[d, par] = src[...].astype(F32)
-        self.K.emit(self.R, buf.at[d, par], h, d, k, self.C.lsem.at[4 + kind * 4 + d * 2 + par])
-
-    def finish(self):
-        R, C, n = self.R, self.C, self.K.n
-
-        def one(k):
-            for d in range(2):
-                i = d * n + k
-                pos = C.z if d == 0 else 3 - C.z
-                fn = R.FN.at[d, k]
-                C.rc(fn, fn, self.a + i, C.xp).wait_send()
-                C.rc(fn, fn, self.x + i, C.xp).wait_send()
-
-                @pl.when(jnp.logical_or(pos == 1, pos == 2))
-                def _():
-                    C.rc(fn, fn, self.b + i, C.xp).wait_send()
-
-        loop(n, one)
-        for d in range(2):
-            for par in range(2):
-                self.slot(R.SF, d, par, 0).wait()
-                self.slot(R.SX, d, par, 1).wait()
+                away(fn, i, 3).start()
+
+            C.rc(fn, R.XH.at[d, kf], one + 4 + d, C.xp).start()
+            pltpu.make_async_copy(fn, R.FH.at[d, kf], C.lsem.at[4 + d]).start()
 
 
 def small_tensor(R, C):
@@ -903,6 +895,8 @@
 
 
 LAG = 3
+LAG_Q = 2
+T_U, T_OWN, T_DA, T_DO, T_KV, T_QB, T_QG = 3, 2, 3, 4, 3, 2, 1
 
 
 def body(names, n, *refs):
@@ -922,53 +916,170 @@
     R.sm[...] = jnp.zeros_like(R.sm)
     R.sm2[...] = jnp.zeros_like(R.sm2)
     R.sd[...] = jnp.zeros_like(R.sd)
-    stage_qkv(R, C)
     pl.semaphore_wait(sem, count)
-    all_to_all(R, C, R.asend, R.arecv, n)()
+    wait_qkv = stage_qkv(R, C, n)
+    wait_qkv()
+    wait_cot = swap_cot(R, C)
     stage_attend(R, C, n)
+    wait_cot()
     stage_out(R, C)
     for cp in wcp:
         cp.wait()
     stage_moe(R, C)
     K = Kinds(half // 32, R.H2.shape[2] // 64)
-    ring = Ring(R, C, K, LAG)
+    sums = Sums(R, C, K.n)
+    ring = Ring(sums, 0, K.q0, LAG)
+    last = Ring(sums, K.q0, K.n, LAG_Q)
     wait_u = reduce8(R, C, R.YP, R.ly, R.sy, R.u)
     wait_x = reduce8(R, C, R.DXP, R.lx, R.sx, R.dx)
     stage_moe_grads(R, C, K, ring)
     wait_u()
-    ring.run(2)
+    ring.run(T_U)
     wait_x()
     stage_owner(R, C)
     wait_da = gather4(R, C, R.DA)
     wait_res = gather4(R, C, R.RES)
-    ring.run(3)
+    ring.run(T_OWN + T_DA)
     wait_da()
     stage_out_back(R, C, n)
     wait_do = all_to_all(R, C, R.osend, R.dorecv, n)
     stage_out_grad(R, C)
     xo = C.send(R.A.at[:, 0:128, :], R.wi.at[:, 0:128, :], C.sems(1), C.xp)
-    ring.run(3)
+    ring.run(T_DO)
     wait_do()
     C.drain()
-    stage_attend_back(R, C, n, ring)
+    stage_attend_back(R, C, n, ring, xo)
     stage_qkv_back(R, C)
     wait_gin = gather4(R, C, R.GIN)
     small = small_tensor(R, C)
-    ring.run(2)
-    xq = stage_qkv_grad(R, C)
+    ring.run(T_QB)
+    xq = stage_qkv_grad(R, C, ring)
     small = small_dp(R, C, n, small)
-    xo.wait_recv()
-    add_tail(R, 0, 2)
-    ring.run(K.o0 - ring.cur)
     for cp in xq:
         cp.wait_recv()
     add_tail(R, 2, 6)
+    for r in range(8):
+        last.run(1)
+        if ring.cur < ring.total:
+            ring.run(1)
     wait_gin()
     wait_res()
-    ring.run(ring.total - ring.cur)
     small_end(R, C, n, small)
-    ring.finish()
+    ring.rest()
+    last.rest()
+    sums.finish()
     C.drain()
+
+
+def place_body(nb, ni, fh, xh, res, gin, osm, oB, oI, oQ, oO, oR, oG, *rest):
+    vec, (cf, cx, cr, cg, vB, vI, vQ, vO, vR, vG, isem, osem) = rest[:9], rest[9:]
+    x = lax.rem(lax.axis_index("dp"), 2)
+    n = nb + ni + 8
+    half = nb * 32
+    cuts = ((0, nb), (nb, ni), (nb + ni, 8))
+    srcs = ((fh, cf, x), (xh, cx, 1 - x))
+    ins = {}
+    for j, (src, buf, h) in enumerate(srcs):
+        for d in range(2):
+            for c, (k0, m) in enumerate(cuts):
+                cp = pltpu.make_async_copy(
+                    src.at[d, pl.ds(k0, m)], buf.at[d, pl.ds(k0, m)], isem.at[j * 6 + d * 3 + c]
+                )
+                cp.start()
+                ins[j, d, c] = cp
+    rows = [pltpu.make_async_copy(a, b, isem.at[12 + i]) for i, (a, b) in enumerate(((res, cr), (gin, cg)))]
+    for cp in rows:
+        cp.start()
+    outs = []
+
+    def put(src, dst):
+        cp = pltpu.make_async_copy(src, dst, osem.at[len(outs)])
+        cp.start()
+        outs.append(cp)
+
+    for j, (src, buf, h) in enumerate(srcs):
+        for d in range(2):
+            ins[j, d, 0].wait()
+
+            def back(k):
+                v = buf[d, k].astype(F32)
+                at = pl.ds(al(k * 32, 32), 32)
+                vB[j, d, at, 0:512] = v[0:32]
+                vB[j, d, at, 512:1024] = v[32:64]
+
+            loop(nb, back)
+            put(vB.at[j, d], oB.at[d, pl.ds(al(h * half, half), half), :])
+            ins[j, d, 1].wait()
+
+            def into(k):
+                vI[j, d, pl.ds(al(k * 64, 64), 64), :] = buf[d, nb + k].astype(F32)
+
+            loop(ni, into)
+            put(vI.at[j, d], oI.at[d, :, pl.ds(al(h * 512, 512), 512)])
+    for j, (src, buf, h) in enumerate(srcs):
+        for d in range(2):
+            ins[j, d, 2].wait()
+            for c in range(2):
+                v = buf[d, nb + ni + c].astype(F32)
+                at = pl.ds(al(h * 128 + d * 64 + c * 32, 32), 32)
+                vO[at, 0:512] = v[0:32]
+                vO[at, 512:1024] = v[32:64]
+            for c in range(6):
+                v = buf[d, nb + ni + 2 + c].astype(F32)
+                row = h * 512 + d * 256 + (c % 2) * 128
+                vQ[c // 2, pl.ds(al(row, 64), 64), :] = v[:, 0:256]
+                vQ[c // 2, pl.ds(al(row + 64, 64), 64), :] = v[:, 256:512]
+    put(vO, oO)
+    put(vQ, oQ)
+    for cp, src, buf, out in ((rows[0], cr, vR, oR), (rows[1], cg, vG, oG)):
+        cp.wait()
+        for t in range(src.shape[0]):
+            buf[t] = src[t].astype(F32)
+        put(buf, out)
+    ln1g, ln1b, qv, outb, ln2g, ln2b, rout, inb, bb = vec
+    for ref, r in ((ln1g, 8), (ln1b, 9), (outb, 2), (ln2g, 0), (ln2b, 1)):
+        ref[...] = osm[r : r + 1, :]
+    for i in range(2):
+        qv[i : i + 1, :] = osm[10:11, i * 256 : i * 256 + 256]
+        rout[i : i + 1, :] = osm[3 + i : 4 + i, :]
+        bb[i : i + 1, :] = osm[5 + i : 6 + i, :]
+        for e in range(2):
+            inb[e : e + 1, i * 512 : i * 512 + 512] = osm[11 + i : 12 + i, e * 512 : e * 512 + 512]
+    for cp in outs:
+        cp.wait()
+
+
+def place(fh, xh, res, gin, osm, nb, ni):
+    sds = jax.ShapeDtypeStruct
+    vm = pl.BlockSpec(memory_space=pltpu.VMEM)
+    hbm = pl.BlockSpec(memory_space=pl.ANY)
+    n, half = nb + ni + 8, nb * 32
+    big = [(2, 2 * half, 1024), (2, ni * 64, 1024), (3, 1024, 256), (256, 1024), res.shape, gin.shape]
+    row = (1, 1024)
+    small = [row, row, (2, 256), row, row, row, (2, 1024), (2, 1024), (2, 1024)]
+    V = pltpu.VMEM
+    return pl.pallas_call(
+        functools.partial(place_body, nb, ni),
+        out_shape=[sds(v, F32) for v in big + small],
+        in_specs=[hbm, hbm, hbm, hbm, vm],
+        out_specs=[hbm] * len(big) + [vm] * len(small),
+        scratch_shapes=[
+            V((2, n, 64, 512), BF),
+            V((2, n, 64, 512), BF),
+            V(res.shape, BF),
+            V(gin.shape, BF),
+            V((2, 2, half, 1024), F32),
+            V((2, 2, ni * 64, 512), F32),
+            V((3, 1024, 256), F32),
+            V((256, 1024), F32),
+            V(res.shape, F32),
+            V(gin.shape, F32),
+            pltpu.SemaphoreType.DMA((14,)),
+            pltpu.SemaphoreType.DMA((12,)),
+        ],
+        compiler_params=pltpu.CompilerParams(vmem_limit_bytes=60000000),
+        name="place",
+    )(fh, xh, res, gin, osm)
 
 
 def fast_local(args, n, nt):
@@ -1003,10 +1114,7 @@
     outs = [
         ("RES", sds((nt, CH, D), BF), vm),
         ("GIN", sds((nt, CH, D), BF), vm),
-        ("oB", sds((2, H, D), F32), hbm),
-        ("oI", sds((2, D, H), F32), hbm),
-        ("oQ", sds((3, D, F), F32), hbm),
-        ("oO", sds((F, D), F32), hbm),
+        ("FH", sds((2, nch, 64, 512), BF), hbm),
         ("XH", sds((2, nch, 64, 512), BF), hbm),
         ("osm", sds((16, D), F32), vm),
     ]
@@ -1035,6 +1143,7 @@
         ("H2", V((8, CH, D), BF)),
         ("GG", V((8, CH, D), BF)),
         ("META", V((8, CH, 128), BF)),
+        ("cx", V((rows, D), BF)),
         ("wi", V((2, D, half), BF)),
         ("wb", V((2, half, D), BF)),
         ("A", V((2, 8 * CH, half), BF)),
@@ -1049,18 +1158,16 @@
         ("G", V((2, nch, 64, 512), BF)),
         ("L1", V((2, nch, 64, 512), BF)),
         ("FN", V((2, nch, 64, 512), BF)),
-        ("SF", V((2, 2, 64, 512), F32)),
-        ("SX", V((2, 2, 64, 512), F32)),
         ("sm", V((8, D), F32)),
         ("sm2", V((8, D), F32)),
         ("st", V((4, 16, D), F32)),
         ("sd", V((n, 16, D), F32)),
-        ("ssem", pltpu.SemaphoreType.DMA((128 + 6 * nch,))),
-        ("rsem", pltpu.SemaphoreType.DMA((128 + 6 * nch,))),
+        ("ssem", pltpu.SemaphoreType.DMA((140 + 4 * nch,))),
+        ("rsem", pltpu.SemaphoreType.DMA((140 + 4 * nch,))),
         ("lsem", pltpu.SemaphoreType.DMA((16,))),
     ]
     names = [i[0] for i in ins] + [o[0] for o in outs] + [s[0] for s in scr]
-    res, gin, oB, oI, oQ, oO, _, osm = pl.pallas_call(
+    res, gin, fh, xh, osm = pl.pallas_call(
         functools.partial(body, names, n),
         out_shape=[o[1] for o in outs],
         in_specs=[i[2] for i in ins],
@@ -1071,23 +1178,25 @@
         ),
         name="layer",
     )(*[i[1] for i in ins])
-    inb = jnp.stack([osm[11].reshape(2, half), osm[12].reshape(2, half)], axis=1).reshape(2, H)
+    oB, oI, oQ, oO, oR, oG, ln1g, ln1b, qv, outb, ln2g, ln2b, rout, inb, bb = place(
+        fh, xh, res, gin, osm, half // 32, D // 64
+    )
     return (
-        res.reshape(S, span, D).astype(F32),
-        gin.reshape(S, span, D).astype(F32),
-        osm[8],
-        osm[9],
+        oR.reshape(S, span, D),
+        oG.reshape(S, span, D),
+        ln1g.reshape(D),
+        ln1b.reshape(D),
         oQ.transpose(1, 0, 2),
-        osm[10, : 2 * F].reshape(2, F),
+        qv,
         oO,
-        osm[2],
-        osm[0],
-        osm[1],
-        osm[3:5].T,
+        outb.reshape(D),
+        ln2g.reshape(D),
+        ln2b.reshape(D),
+        rout.T,
         oI,
         inb,
         oB,
-        osm[5:7],
+        bb,
     )
 
 

time: 333 us -> 307 us (0.922)
  local copies, waits for them, and re-layouts: 23.4 us -> 4.98 us
  other arithmetic: 5.35 us -> 0.64 us
    pallas_call x1, Pallas kernels: 302 us -> 286 us  [fast_local(): pl.pallas_call(functools.partial(body, names, n), out_shape=[o[1] for o i...]
    unnamed x14 -> x0, local copies, waits for them, and re-layouts: 13.9 us -> none
    pallas_call x0 -> x1, Pallas kernels: none -> 13.6 us  [place(): pl.pallas_call(functools.partial(place_body, nb, ni), out_shape=[sds(v, F...]
    convert_element_type x1 -> x0, other arithmetic: 4.1 us -> none  [fast_local(): gin.reshape(S, span, D).astype(F32)]
    slice x3 -> x0, local copies, waits for them, and re-layouts: 3.88 us -> none  [the longest x1 1.56 us: fast_local(): osm[11].reshape(2, half)]
where the time goes in v3:
time: 307 us; the launch traced here: 306 us
  Pallas kernels  300 us (98%)
  local copies, waits for them, and re-layouts  4.98 us (2%)
    pallas_call x1, Pallas kernels, fast_local(): pl.pallas_call(functools.partial(body, names, n), out_shape=[o[1] for o i...  286 us
    pallas_call x1, Pallas kernels, place(): pl.pallas_call(functools.partial(place_body, nb, ni), out_shape=[sds(v, F...  13.6 us

profile of v3, /device:TPU:0, one launch (start us, length us, event | category | flops | bytes accessed | tf_op | source)
XLA Modules:
  0.0 306.3 jit_solution(6750833798273017775)
XLA Ops:
  0.6 0.7 stack.15
  1.3 0.7 stack.16
  2.0 0.7 stack.17
  2.7 0.7 stack.18
  3.4 0.7 stack.19
  4.1 1.6 concatenate.3
  5.6 0.6 convert_element_type.3.refs_1_
  6.3 286.3 %layer.1 = (bf16[4,128,1024]{2,1,0:T(8,128)(2,1)}, bf16[4,128,1024]{2,1,0:T(8,128)(2,1)}, bf16[2,40,64,512]{3,2,1,0:T(8,128)(2,1)}, bf16[2,40,64,512]{3,2,1,0:T(8,128)(2,1)}, f32[16,1024]{1,0:T(8,128)}) custom-call(bf16[512,1024]{1,0:T(8,128)(2,1)} %bitcast.15, f32[16,1024]{1,0:T(8,128)} %convert_element_type.3.refs_1_, bf16[3,1024,256]{2,1,0:T(8,128)(2,1)} %bitcast.14, ...), custom_call_target="tpu_custom_call" | custom-call | tf_op jit(solution)/shard_map/layer/pallas_call | solution.py:1170
  292.5 13.6 %place.1 = (f32[2,1024,1024]{2,1,0:T(8,128)}, f32[2,1024,1024]{2,1,0:T(8,128)}, f32[3,1024,256]{2,1,0:T(8,128)}, f32[256,1024]{1,0:T(8,128)}, f32[4,128,1024]{2,...) custom-call(bf16[2,40,64,512]{3,2,1,0:T(8,128)(2,1)} %get-tuple-elem, ...), custom_call_target="tpu_custom_call" | custom-call | tf_op jit(solution)/shard_map/place/pallas_call | solution.py:1061
  (1 shorter events, 0.0 us)

commit v4 on v3

--- a/solution.py
+++ b/solution.py
@@ -283,7 +283,7 @@
     return wait
 
 
-def reduce4(R, C, part, out):
+def reduce4(R, C, part, out, fill=lambda: None):
     k = C.sems(3)
     k0 = (1 - C.y) * 2 + (1 - C.c)
     k1 = (1 - C.y) * 2 + C.c
@@ -291,12 +291,14 @@
     R.p4[0] = part(k0).astype(BF)
     c0 = C.send(R.p4.at[0], R.l4.at[0], k, C.mate)
     v1 = part(k1)
+    fill()
     c0.wait_recv()
     R.p4[1] = (v1 + R.l4[0].astype(F32)).astype(BF)
     c1 = C.send(R.p4.at[1], R.l4.at[2], k + 1, C.yp)
     R.p4[2] = part(k2).astype(BF)
     c2 = C.send(R.p4.at[2], R.l4.at[1], k + 2, C.mate)
     out[...] = part(C.t)
+    fill()
     c2.wait_recv()
     c1.wait_recv()
     out[...] = out[...] + R.l4[1].astype(F32) + R.l4[2].astype(F32)
@@ -607,11 +609,11 @@
     R.dq[...] = jnp.zeros_like(R.dq)
     k = C.sems(n)
     k2 = C.sems(n)
-    base = ring.take(2 * nt)
+    base = ring.take(T_AB * nt)
     kvs, kvr, dqr = R.asend.at[:, 0:256], R.arecv.at[:, 0:256], R.arecv.at[:, 256:384]
 
     def keys(jj):
-        ring.tick(base + 2 * jj)
+        loop(T_AB // 2, lambda i: ring.tick(base + T_AB * jj + i))
         j = nt - 1 - jj
         kat = pl.ds(al(j * T, T), T)
         kk, vv = R.K[kat, :], R.V[kat, :]
@@ -644,7 +646,7 @@
             def _():
                 C.rc(kvs.at[b], kvr.at[C.dp], k + b, (b, C.t), k + C.dp).start()
 
-        ring.tick(base + 2 * jj + 1)
+        loop(T_AB - T_AB // 2, lambda i: ring.tick(base + T_AB * jj + T_AB // 2 + i))
 
     loop(nt, keys)
 
@@ -687,7 +689,7 @@
     unfold_heads(dqr, R.dproj.at[0], n, seqs)
 
 
-def stage_qkv_back(R, C):
+def stage_qkv_back(R, C, fill):
     def part(k):
         at = pl.ds(al(k * CH, CH), CH)
         return (
@@ -696,7 +698,7 @@
             + mm_bt(R.dproj[2, at, :], R.wqkv[2])
         )
 
-    reduce4(R, C, part, R.dx)
+    reduce4(R, C, part, R.dx, fill)
     own = pl.ds(al(C.t * CH, CH), CH)
     n, r = norm_parts(R.tok[own, :].astype(F32))
     dh1 = R.dx[...]
@@ -771,6 +773,9 @@
         return base
 
     def run(self, n):
+        n = min(n, self.total - self.cur)
+        if n <= 0:
+            return
         base = self.take(n)
         loop(n, lambda i: self.tick(base + i))
 
@@ -896,7 +901,7 @@
 
 LAG = 3
 LAG_Q = 2
-T_U, T_OWN, T_DA, T_DO, T_KV, T_QB, T_QG = 3, 2, 3, 4, 3, 2, 1
+T_U, T_DA, T_DO, T_AB, T_KV, T_QB, T_QG = 3, 5, 4, 2, 3, 2, 1
 
 
 def body(names, n, *refs):
@@ -913,6 +918,10 @@
     ]
     for cp in wcp:
         cp.start()
+    for i, ref in enumerate((R.g1, R.b1, R.outb, R.g2, R.b2)):
+        R.par[i : i + 1, :] = ref[...].astype(F32).reshape(1, ref.shape[0])
+    R.par[5:7, :] = R.router[...].astype(F32)
+    R.par[7:9, :] = R.backb[...].astype(F32)
     R.sm[...] = jnp.zeros_like(R.sm)
     R.sm2[...] = jnp.zeros_like(R.sm2)
     R.sd[...] = jnp.zeros_like(R.sd)
@@ -939,7 +948,7 @@
     stage_owner(R, C)
     wait_da = gather4(R, C, R.DA)
     wait_res = gather4(R, C, R.RES)
-    ring.run(T_OWN + T_DA)
+    ring.run(T_DA)
     wait_da()
     stage_out_back(R, C, n)
     wait_do = all_to_all(R, C, R.osend, R.dorecv, n)
@@ -949,19 +958,18 @@
     wait_do()
     C.drain()
     stage_attend_back(R, C, n, ring, xo)
-    stage_qkv_back(R, C)
+    xq = stage_qkv_grad(R, C, ring)
+    stage_qkv_back(R, C, lambda: ring.run(T_QB))
     wait_gin = gather4(R, C, R.GIN)
     small = small_tensor(R, C)
-    ring.run(T_QB)
-    xq = stage_qkv_grad(R, C, ring)
-    small = small_dp(R, C, n, small)
     for cp in xq:
         cp.wait_recv()
     add_tail(R, 2, 6)
     for r in range(8):
         last.run(1)
-        if ring.cur < ring.total:
-            ring.run(1)
+        ring.run(1)
+        if r == 2:
+            small = small_dp(R, C, n, small)
     wait_gin()
     wait_res()
     small_end(R, C, n, small)
@@ -1091,14 +1099,17 @@
     H = w_in.shape[2]
     half = H // 2
     total = n * span
-    par = jnp.concatenate(
-        [jnp.stack([g1, b1, out_b, g2, b2]), router.T, back_b, jnp.zeros((7, D), BF)], axis=0
-    ).astype(F32)
     vm = pl.BlockSpec(memory_space=pltpu.VMEM)
     hbm = pl.BlockSpec(memory_space=pl.ANY)
     ins = [
         ("tok", tokens.reshape(rows, D), vm),
-        ("par", par, vm),
+        ("g1", g1, vm),
+        ("b1", b1, vm),
+        ("outb", out_b, vm),
+        ("g2", g2, vm),
+        ("b2", b2, vm),
+        ("router", router.T, vm),
+        ("backb", back_b, vm),
         ("wqkv", w_qkv.transpose(1, 0, 2), vm),
         ("qvb", qvb, vm),
         ("wout", w_out, vm),
@@ -1144,6 +1155,7 @@
         ("GG", V((8, CH, D), BF)),
         ("META", V((8, CH, 128), BF)),
         ("cx", V((rows, D), BF)),
+        ("par", V((16, D), F32)),
         ("wi", V((2, D, half), BF)),
         ("wb", V((2, half, D), BF)),
         ("A", V((2, 8 * CH, half), BF)),

time: 307 us -> 288 us (0.938)
  Pallas kernels: 300 us -> 287 us
  local copies, waits for them, and re-layouts: 4.98 us -> 0 us
    pallas_call x1, Pallas kernels: 286 us -> 273 us  [fast_local(): pl.pallas_call(functools.partial(body, names, n), out_shape=[o[1] for o i...]
    another operation x5 -> x0, local copies, waits for them, and re-layouts: 3.43 us -> none  [fast_local(): jnp.stack([g1, b1, out_b, g2, b2])]
where the time goes in v4:
time: 288 us; the launch traced here: 287 us
  Pallas kernels  287 us (100%)
    pallas_call x1, Pallas kernels, fast_local(): pl.pallas_call(functools.partial(body, names, n), out_shape=[o[1] for o i...  273 us
    pallas_call x1, Pallas kernels, place(): pl.pallas_call(functools.partial(place_body, nb, ni), out_shape=[sds(v, F...  13.6 us

profile of v4, /device:TPU:0, one launch (start us, length us, event | category | flops | bytes accessed | tf_op | source)
XLA Modules:
  0.0 287.4 jit_solution(8816216058690403850)
XLA Ops:
  0.7 273.1 %layer.1 = (bf16[4,128,1024]{2,1,0:T(8,128)(2,1)}, bf16[4,128,1024]{2,1,0:T(8,128)(2,1)}, bf16[2,40,64,512]{3,2,1,0:T(8,128)(2,1)}, bf16[2,40,64,512]{3,2,1,0:T(8,128)(2,1)}, f32[16,1024]{1,0:T(8,128)}) custom-call(bf16[512,1024]{1,0:T(8,128)(2,1)} %bitcast.15, bf16[1024]{0:T(1024)(128)(2,1)} %refs_1_.1, bf16[1024]{0:T(1024)(128)(2,1)} %refs_2_.1, ...), custom_call_target="tpu_custom_call" | custom-call | tf_op jit(solution)/shard_map/layer/pallas_call | solution.py:1182
  273.7 13.6 %place.1 = (f32[2,1024,1024]{2,1,0:T(8,128)}, f32[2,1024,1024]{2,1,0:T(8,128)}, f32[3,1024,256]{2,1,0:T(8,128)}, f32[256,1024]{1,0:T(8,128)}, f32[4,128,1024]{2,...) custom-call(bf16[2,40,64,512]{3,2,1,0:T(8,128)(2,1)} %get-tuple-elem, ...), custom_call_target="tpu_custom_call" | custom-call | tf_op jit(solution)/shard_map/place/pallas_call | solution.py:1069

commit v5 on v4

--- a/solution.py
+++ b/solution.py
@@ -406,8 +406,57 @@
     return h * half, half + h * (jnp.exp(-0.5 * h * h) * 0.3989422804014327)
 
 
-def stage_moe(R, C):
-    def tile(i):
+class Reduce8:
+    def __init__(self, C, parts, land, stage, out):
+        self.C, self.parts, self.land, self.stage, self.out = C, parts, land, stage, out
+        self.k = C.sems(7)
+
+    def place(self, n):
+        C = self.C
+        a, b = n // 2, lax.rem(n, 2)
+        xx = (1 - C.x) * (1 - a) + C.x * a
+        yy = (1 - C.y) * (1 - b) + C.y * b
+        return xx, yy
+
+    def swap(self, n):
+        C = self.C
+        xx, yy = self.place(n)
+        src = self.parts.at[xx * 4 + yy * 2 + 1 - C.c]
+        return C.rc(src, self.land.at[n], self.k + n, C.mate)
+
+    def added(self, n):
+        C = self.C
+        xx, yy = self.place(n)
+        self.swap(n).wait_recv()
+        return self.parts[xx * 4 + yy * 2 + C.c].astype(F32) + self.land[n].astype(F32)
+
+    def cross(self, n):
+        C = self.C
+        xx, yy = self.place(n)
+        dev = (C.z * 2 + xx, yy * 2 + C.c)
+        return C.rc(self.stage.at[n], self.land.at[4 + n], self.k + 4 + n, dev)
+
+    def forward(self, n):
+        self.stage[n] = self.added(n).astype(BF)
+        self.cross(n).start()
+
+    def keep(self):
+        self.out[...] = self.added(3)
+        self.C.pending += [self.swap(n) for n in range(4)] + [self.cross(n) for n in range(3)]
+
+    def wait(self):
+        for n in range(3):
+            self.cross(n).wait_recv()
+        v = self.out[...]
+        for n in range(3):
+            v = v + self.land[4 + n].astype(F32)
+        self.out[...] = v
+
+
+def stage_moe(R, C, sums):
+    def tile(n):
+        xx, yy = sums[0].place(n)
+        i = xx * 2 + yy
         two = pl.ds(al(2 * i, 2), 2)
         at = pl.ds(al(i * 256, 256), 256)
         h2 = R.H2[two].reshape(256, R.H2.shape[2])
@@ -433,8 +482,17 @@
         R.YP[two] = y.astype(BF).reshape(2, CH, y.shape[1])
         dx = mm_bt(R.DH[0, at, :], R.wi[0]) + mm_bt(R.DH[1, at, :], R.wi[1])
         R.DXP[two] = dx.astype(BF).reshape(2, CH, dx.shape[1])
+        for r in sums:
+            r.swap(n).start()
+
+        @pl.when(n > 0)
+        def _():
+            for r in sums:
+                r.forward(n - 1)
 
     loop(4, tile)
+    for r in sums:
+        r.keep()
 
 
 def put_wide(at, v):
@@ -471,33 +529,6 @@
             ring.tick(base + i // 2)
 
     loop(R.H2.shape[2] // 128, into)
-
-
-def reduce8(R, C, parts, land, stage, out):
-    k = C.sems(7)
-    order = ((1 - C.x, 1 - C.y), (1 - C.x, C.y), (C.x, 1 - C.y), (C.x, C.y))
-    devs = (C.dg, C.xp, C.yp)
-    cm = []
-    for n, (xx, yy) in enumerate(order):
-        cm.append(C.send(parts.at[xx * 4 + yy * 2 + 1 - C.c], land.at[n], k + n, C.mate))
-    cr = []
-    for n, (xx, yy) in enumerate(order):
-        cm[n].wait_recv()
-        v = parts[xx * 4 + yy * 2 + C.c].astype(F32) + land[n].astype(F32)
-        if n < 3:
-            stage[n] = v.astype(BF)
-            cr.append(C.send(stage.at[n], land.at[4 + n], k + 4 + n, devs[n]))
-        else:
-            out[...] = v
-
-    def wait():
-        for n in range(3):
-            cr[n].wait_recv()
-        out[...] = (
-            out[...] + land[4].astype(F32) + land[5].astype(F32) + land[6].astype(F32)
-        )
-
-    return wait
 
 
 def norm_back(n, r, dn):
@@ -901,7 +932,7 @@
 
 LAG = 3
 LAG_Q = 2
-T_U, T_DA, T_DO, T_AB, T_KV, T_QB, T_QG = 3, 5, 4, 2, 3, 2, 1
+T_U, T_DA, T_DO, T_AB, T_KV, T_QB, T_QG = 3, 5, 4, 2, 4, 3, 1
 
 
 def body(names, n, *refs):
@@ -934,17 +965,17 @@
     stage_out(R, C)
     for cp in wcp:
         cp.wait()
-    stage_moe(R, C)
+    over_u = Reduce8(C, R.YP, R.ly, R.sy, R.u)
+    over_x = Reduce8(C, R.DXP, R.lx, R.sx, R.dx)
+    stage_moe(R, C, (over_u, over_x))
     K = Kinds(half // 32, R.H2.shape[2] // 64)
     sums = Sums(R, C, K.n)
     ring = Ring(sums, 0, K.q0, LAG)
     last = Ring(sums, K.q0, K.n, LAG_Q)
-    wait_u = reduce8(R, C, R.YP, R.ly, R.sy, R.u)
-    wait_x = reduce8(R, C, R.DXP, R.lx, R.sx, R.dx)
     stage_moe_grads(R, C, K, ring)
-    wait_u()
+    over_u.wait()
     ring.run(T_U)
-    wait_x()
+    over_x.wait()
     stage_owner(R, C)
     wait_da = gather4(R, C, R.DA)
     wait_res = gather4(R, C, R.RES)
@@ -953,10 +984,10 @@
     stage_out_back(R, C, n)
     wait_do = all_to_all(R, C, R.osend, R.dorecv, n)
     stage_out_grad(R, C)
-    xo = C.send(R.A.at[:, 0:128, :], R.wi.at[:, 0:128, :], C.sems(1), C.xp)
     ring.run(T_DO)
     wait_do()
     C.drain()
+    xo = C.send(R.A.at[:, 0:128, :], R.wi.at[:, 0:128, :], C.sems(1), C.xp)
     stage_attend_back(R, C, n, ring, xo)
     xq = stage_qkv_grad(R, C, ring)
     stage_qkv_back(R, C, lambda: ring.run(T_QB))

time: 288 us -> 287 us (level)
  no operation moved by 1% of the time
where the time goes in v5:
time: 287 us
  Pallas kernels  286 us (100%)
    pallas_call x1, Pallas kernels, fast_local(): pl.pallas_call(functools.partial(body, names, n), out_shape=[o[1] for o i...  272 us
    pallas_call x1, Pallas kernels, place(): pl.pallas_call(functools.partial(place_body, nb, ni), out_shape=[sds(v, F...  13.6 us

profile of v5, /device:TPU:0, one launch (start us, length us, event | category | flops | bytes accessed | tf_op | source)
XLA Modules:
  0.0 286.6 jit_solution(4125418425727751106)
XLA Ops:
  0.7 272.2 %layer.1 = (bf16[4,128,1024]{2,1,0:T(8,128)(2,1)}, bf16[4,128,1024]{2,1,0:T(8,128)(2,1)}, bf16[2,40,64,512]{3,2,1,0:T(8,128)(2,1)}, bf16[2,40,64,512]{3,2,1,0:T(8,128)(2,1)}, f32[16,1024]{1,0:T(8,128)}) custom-call(bf16[512,1024]{1,0:T(8,128)(2,1)} %bitcast.15, bf16[1024]{0:T(1024)(128)(2,1)} %refs_1_.1, bf16[1024]{0:T(1024)(128)(2,1)} %refs_2_.1, ...), custom_call_target="tpu_custom_call" | custom-call | tf_op jit(solution)/shard_map/layer/pallas_call | solution.py:1213
  272.9 13.6 %place.1 = (f32[2,1024,1024]{2,1,0:T(8,128)}, f32[2,1024,1024]{2,1,0:T(8,128)}, f32[3,1024,256]{2,1,0:T(8,128)}, f32[256,1024]{1,0:T(8,128)}, f32[4,128,1024]{2,...) custom-call(bf16[2,40,64,512]{3,2,1,0:T(8,128)(2,1)} %get-tuple-elem, ...), custom_call_target="tpu_custom_call" | custom-call | tf_op jit(solution)/shard_map/place/pallas_call | solution.py:1100

commit v6 on v5

--- a/solution.py
+++ b/solution.py
@@ -770,10 +770,10 @@
 
 
 class Sums:
-    def __init__(self, R, C, n):
-        self.R, self.C, self.n = R, C, n
+    def __init__(self, R, C, n, via):
+        self.R, self.C, self.n, self.via = R, C, n, via
         self.a, self.b = C.sems(2 * n), C.sems(2 * n)
-        self.one = C.sems(6)
+        self.one, self.v = C.sems(10), C.sems(2 * via)
 
     def finish(self):
         R, C = self.R, self.C
@@ -786,9 +786,26 @@
             def _():
                 C.rc(fn, fn, self.one + 2 + d, C.xp).wait_send()
 
-            cp = C.rc(fn, R.XH.at[d], self.one + 4 + d, C.xp)
+            tail, head = pl.ds(self.via, self.n - self.via), pl.ds(0, self.via)
+            cp = C.rc(R.FN.at[d, tail], R.XH.at[d, tail], self.one + 4 + d, C.xp)
             cp.wait_send()
             cp.wait_recv()
+            odd = lax.rem(pos, 2) == 1
+
+            @pl.when(odd)
+            def _():
+                for i in (6, 8):
+                    C.rc(R.FN.at[d, head], R.XH.at[d, head], self.one + i + d, C.xp).wait_send()
+
+            @pl.when(jnp.logical_not(odd))
+            def _():
+                def got(k):
+                    xh = R.XH.at[d, k]
+                    i = self.v + d * self.via + k
+                    C.rc(xh, xh, self.one + 8 + d, C.xp, i).wait_recv()
+
+                loop(self.via, got)
+
             pltpu.make_async_copy(fn, R.FH.at[d], C.lsem.at[4 + d]).wait()
 
 
@@ -863,6 +880,7 @@
 
         lag = w * (2 + jnp.where(pos == 1, 0, 1) + jnp.where(pos == 3, 1, 0))
         kf = s - lag
+        odd = lax.rem(pos, 2) == 1
 
         @pl.when(act(kf, None))
         def _():
@@ -877,8 +895,26 @@
             def _():
                 away(fn, i, 3).start()
 
-            C.rc(fn, R.XH.at[d, kf], one + 4 + d, C.xp).start()
+            @pl.when(kf >= S.via)
+            def _():
+                C.rc(fn, R.XH.at[d, kf], one + 4 + d, C.xp).start()
+
+            @pl.when(jnp.logical_and(kf < S.via, odd))
+            def _():
+                i = S.v + d * S.via + kf
+                C.rc(fn, R.XH.at[d, kf], one + 6 + d, C.xp, i).start()
+
             pltpu.make_async_copy(fn, R.FH.at[d, kf], C.lsem.at[4 + d]).start()
+
+        if self.k0 < S.via:
+            kv = kf - w
+
+            @pl.when(act(kv, jnp.logical_and(odd, kv < S.via)))
+            def _():
+                xh = R.XH.at[d, kv]
+                cp = C.rc(xh, xh, one + 8 + d, dev(pos - 1), S.v + d * S.via + kv)
+                cp.wait_recv()
+                cp.start()
 
 
 def small_tensor(R, C):
@@ -969,7 +1005,7 @@
     over_x = Reduce8(C, R.DXP, R.lx, R.sx, R.dx)
     stage_moe(R, C, (over_u, over_x))
     K = Kinds(half // 32, R.H2.shape[2] // 64)
-    sums = Sums(R, C, K.n)
+    sums = Sums(R, C, K.n, K.i0)
     ring = Ring(sums, 0, K.q0, LAG)
     last = Ring(sums, K.q0, K.n, LAG_Q)
     stage_moe_grads(R, C, K, ring)
@@ -1205,8 +1241,8 @@
         ("sm2", V((8, D), F32)),
         ("st", V((4, 16, D), F32)),
         ("sd", V((n, 16, D), F32)),
-        ("ssem", pltpu.SemaphoreType.DMA((140 + 4 * nch,))),
-        ("rsem", pltpu.SemaphoreType.DMA((140 + 4 * nch,))),
+        ("ssem", pltpu.SemaphoreType.DMA((180 + 4 * nch,))),
+        ("rsem", pltpu.SemaphoreType.DMA((180 + 4 * nch,))),
         ("lsem", pltpu.SemaphoreType.DMA((16,))),
     ]
     names = [i[0] for i in ins] + [o[0] for o in outs] + [s[0] for s in scr]

time: 287 us -> 304 us (1.059)
  Pallas kernels: 286 us -> 301 us
    pallas_call x1, Pallas kernels: 272 us -> 288 us  [fast_local(): pl.pallas_call(functools.partial(body, names, n), out_shape=[o[1] for o i...]
where the time goes in v6:
time: 304 us; the launch traced here: 302 us
  Pallas kernels  301 us (99%)
    pallas_call x1, Pallas kernels, fast_local(): pl.pallas_call(functools.partial(body, names, n), out_shape=[o[1] for o i...  288 us
    pallas_call x1, Pallas kernels, place(): pl.pallas_call(functools.partial(place_body, nb, ni), out_shape=[sds(v, F...  13.6 us

profile of v6, /device:TPU:0, one launch (start us, length us, event | category | flops | bytes accessed | tf_op | source)
XLA Modules:
  0.0 302.3 jit_solution(16054522739988230806)
XLA Ops:
  0.7 287.9 %layer.1 = (bf16[4,128,1024]{2,1,0:T(8,128)(2,1)}, bf16[4,128,1024]{2,1,0:T(8,128)(2,1)}, bf16[2,40,64,512]{3,2,1,0:T(8,128)(2,1)}, bf16[2,40,64,512]{3,2,1,0:T(8,128)(2,1)}, f32[16,1024]{1,0:T(8,128)}) custom-call(bf16[512,1024]{1,0:T(8,128)(2,1)} %bitcast.15, bf16[1024]{0:T(1024)(128)(2,1)} %refs_1_.1, bf16[1024]{0:T(1024)(128)(2,1)} %refs_2_.1, ...), custom_call_target="tpu_custom_call" | custom-call | tf_op jit(solution)/shard_map/layer/pallas_call | solution.py:1249
  288.6 13.6 %place.1 = (f32[2,1024,1024]{2,1,0:T(8,128)}, f32[2,1024,1024]{2,1,0:T(8,128)}, f32[3,1024,256]{2,1,0:T(8,128)}, f32[256,1024]{1,0:T(8,128)}, f32[4,128,1024]{2,...) custom-call(bf16[2,40,64,512]{3,2,1,0:T(8,128)(2,1)} %get-tuple-elem, ...), custom_call_target="tpu_custom_call" | custom-call | tf_op jit(solution)/shard_map/place/pallas_call | solution.py:1136

commit v7 on v5

--- a/solution.py
+++ b/solution.py
@@ -773,18 +773,32 @@
     def __init__(self, R, C, n):
         self.R, self.C, self.n = R, C, n
         self.a, self.b = C.sems(2 * n), C.sems(2 * n)
-        self.one = C.sems(6)
-
-    def finish(self):
+        self.one = C.sems(10)
+
+    def finish(self, cut):
         R, C = self.R, self.C
         for d in range(2):
             pos = C.z if d == 0 else 3 - C.z
             fn = R.FN.at[d]
-            C.rc(fn, fn, self.one + d, C.xp).wait_send()
+
+            def sent(k0, m, i):
+                part = R.FN.at[d, pl.ds(k0, m)]
+                C.rc(part, part, self.one + i + d, C.xp).wait_send()
+
+            rest = self.n - cut
+            sent(cut, rest, 0)
 
             @pl.when(jnp.logical_or(pos == 1, pos == 2))
             def _():
-                C.rc(fn, fn, self.one + 2 + d, C.xp).wait_send()
+                sent(cut, rest, 2)
+
+            @pl.when(pos < 3)
+            def _():
+                sent(0, cut, 6)
+
+            @pl.when(pos > 0)
+            def _():
+                sent(0, cut, 8)
 
             cp = C.rc(fn, R.XH.at[d], self.one + 4 + d, C.xp)
             cp.wait_send()
@@ -876,6 +890,69 @@
             @pl.when(pos == 2)
             def _():
                 away(fn, i, 3).start()
+
+            C.rc(fn, R.XH.at[d, kf], one + 4 + d, C.xp).start()
+            pltpu.make_async_copy(fn, R.FH.at[d, kf], C.lsem.at[4 + d]).start()
+
+
+class Chain(Ring):
+    def __init__(self, sums, k0, k1, w):
+        super().__init__(sums, k0, k1, w)
+        self.total = k1 - k0 + 6 * w
+
+    def half(self, s, d):
+        S, w = self.S, self.w
+        R, C, n, one = S.R, S.C, S.n, S.one
+        pos = C.z if d == 0 else 3 - C.z
+        step = 1 if d == 0 else -1
+        up = ((C.z + step) * 2 + C.x, C.t)
+        down = ((C.z - step) * 2 + C.x, C.t)
+
+        def act(k, cond):
+            ok = jnp.logical_and(k >= self.k0, k < self.k1)
+            return ok if cond is None else jnp.logical_and(ok, cond)
+
+        def toward(i, k):
+            return C.rc(R.G.at[d, k], R.L1.at[d, k], one + 6 + d, up, S.a + i)
+
+        def away(i, k):
+            return C.rc(R.FN.at[d, k], R.FN.at[d, k], one + 8 + d, down, S.b + i)
+
+        k = s - pos * w
+
+        @pl.when(act(k, pos == 0))
+        def _():
+            toward(d * n + k, k).start()
+
+        @pl.when(act(k, pos > 0))
+        def _():
+            i = d * n + k
+            toward(i, k).wait_recv()
+            v = (R.G[d, k].astype(F32) + R.L1[d, k].astype(F32)).astype(BF)
+
+            @pl.when(pos < 3)
+            def _():
+                R.G[d, k] = v
+                toward(i, k).start()
+
+            @pl.when(pos == 3)
+            def _():
+                R.FN[d, k] = v
+
+        kf = s - (6 - pos) * w
+
+        @pl.when(act(kf, None))
+        def _():
+            i = d * n + kf
+            fn = R.FN.at[d, kf]
+
+            @pl.when(pos < 3)
+            def _():
+                away(i, kf).wait_recv()
+
+            @pl.when(pos > 0)
+            def _():
+                away(i, kf).start()
 
             C.rc(fn, R.XH.at[d, kf], one + 4 + d, C.xp).start()
             pltpu.make_async_copy(fn, R.FH.at[d, kf], C.lsem.at[4 + d]).start()
@@ -930,7 +1007,7 @@
     pass
 
 
-LAG = 3
+LAG = 2
 LAG_Q = 2
 T_U, T_DA, T_DO, T_AB, T_KV, T_QB, T_QG = 3, 5, 4, 2, 4, 3, 1
 
@@ -970,7 +1047,7 @@
     stage_moe(R, C, (over_u, over_x))
     K = Kinds(half // 32, R.H2.shape[2] // 64)
     sums = Sums(R, C, K.n)
-    ring = Ring(sums, 0, K.q0, LAG)
+    ring = Chain(sums, 0, K.q0, LAG)
     last = Ring(sums, K.q0, K.n, LAG_Q)
     stage_moe_grads(R, C, K, ring)
     over_u.wait()
@@ -1006,7 +1083,7 @@
     small_end(R, C, n, small)
     ring.rest()
     last.rest()
-    sums.finish()
+    sums.finish(K.q0)
     C.drain()
 
 

time: 287 us -> 289 us (level)
  no operation moved by 1% of the time
where the time goes in v7:
time: 289 us; the launch traced here: 288 us
  Pallas kernels  288 us (100%)
    pallas_call x1, Pallas kernels, fast_local(): pl.pallas_call(functools.partial(body, names, n), out_shape=[o[1] for o i...  274 us
    pallas_call x1, Pallas kernels, place(): pl.pallas_call(functools.partial(place_body, nb, ni), out_shape=[sds(v, F...  13.6 us

profile of v7, /device:TPU:0, one launch (start us, length us, event | category | flops | bytes accessed | tf_op | source)
XLA Modules:
  0.0 288.4 jit_solution(4562762551432076746)
XLA Ops:
  0.7 274.0 %layer.1 = (bf16[4,128,1024]{2,1,0:T(8,128)(2,1)}, bf16[4,128,1024]{2,1,0:T(8,128)(2,1)}, bf16[2,40,64,512]{3,2,1,0:T(8,128)(2,1)}, bf16[2,40,64,512]{3,2,1,0:T(8,128)(2,1)}, f32[16,1024]{1,0:T(8,128)}) custom-call(bf16[512,1024]{1,0:T(8,128)(2,1)} %bitcast.15, bf16[1024]{0:T(1024)(128)(2,1)} %refs_1_.1, bf16[1024]{0:T(1024)(128)(2,1)} %refs_2_.1, ...), custom_call_target="tpu_custom_call" | custom-call | tf_op jit(solution)/shard_map/layer/pallas_call | solution.py:1290
  274.7 13.6 %place.1 = (f32[2,1024,1024]{2,1,0:T(8,128)}, f32[2,1024,1024]{2,1,0:T(8,128)}, f32[3,1024,256]{2,1,0:T(8,128)}, f32[256,1024]{1,0:T(8,128)}, f32[4,128,1024]{2,...) custom-call(bf16[2,40,64,512]{3,2,1,0:T(8,128)(2,1)} %get-tuple-elem, ...), custom_call_target="tpu_custom_call" | custom-call | tf_op jit(solution)/shard_map/place/pallas_call | solution.py:1177
